TPU v7x, 32 devices: a whole 2x2x4 slice. The times are simulated.
32 devices in a mesh: shot: 4 (over y, core), gx: 4 (over z), gy: 2 (over x).
Axes of the slice: x: 2, y: 2, z: 4, core: 2. Of those that a mesh axis runs over, the one named last changes fastest.
Arguments:
- latent: float32 [32, 24, 1024], P('shot', 'gx', 'gy'), may hold values from -6 to 6
- w_first: float32 [64, 64], replicated, may hold values from -0.75 to 0.75
- w_second: float32 [64, 128], replicated, may hold values from -0.75 to 0.75
- fwd_press: float32 [4, 96, 64, 128], P('shot', 'gx', 'gy'), may hold values from -1.5 to 8
- fwd_vel: float32 [4, 3, 96, 64, 128], P('shot', None, 'gx', 'gy'), may hold values from -1.5 to 8
- adj_press: float32 [4, 96, 64, 128], P('shot', 'gx', 'gy'), may hold values from -1.5 to 8
- adj_vel: float32 [4, 3, 96, 64, 128], P('shot', None, 'gx', 'gy'), may hold values from -1.5 to 8
- src_pos: int32 [3, 4], P(None, 'shot'), may hold values from 0 to 127, as said below
- src_amp: float32 [3, 4], P(None, 'shot'), may hold values from -24 to 24
- rec_pos: int32 [4, 3, 2048], P('shot'), may hold values from 0 to 127, as said below
- observed: float32 [4, 3, 2048], P('shot'), may hold values from -6 to 6
Outputs:
- grad_latent: float32 [32, 24, 1024], P('shot', 'gx', 'gy')
- grad_first: float32 [64, 64], replicated
- grad_second: float32 [64, 128], replicated
Inputs may be any that keep to these rules, and one draw needn't show every extreme that they name: `src_pos`: row 0 is an x cell below 96, row 1 a y cell below 64, row 2 a depth cell below 128. `rec_pos`: component 0 is an x cell below 96, component 1 a y cell below 64, component 2 a depth cell below 128; cells may repeat.
All inputs are finite; a program needn't handle non-finite values.
Results may differ from a plain program's by a relative error of at most 0.0003.
Values sent between devices are 32-bit elements; how exact they have to be, the bound alone decides.
A program may use at most 64 MiB of HBM per device.

v0:
```python
import jax
import jax.numpy as jnp
from jax import lax
from jax.experimental import pallas as pl
from jax.experimental.pallas import tpu as pltpu
from jax.sharding import PartitionSpec as P

CH = 64
STEPS = 3


coeffs = (1225.0 / 1024.0, -245.0 / 3072.0, 49.0 / 5120.0, -5.0 / 7168.0)


def axis_peers(axis, distance):
    count = lax.axis_size(axis)
    return {axis: lax.rem(lax.axis_index(axis) + distance, count)}


def greet(axes):
    barrier = pltpu.get_barrier_semaphore()
    total = 0
    for axis in axes:
        for distance in range(1, lax.axis_size(axis)):
            pl.semaphore_signal(
                barrier,
                inc=1,
                device_id=axis_peers(axis, distance),
                device_id_type=pl.DeviceIdType.MESH,
            )
            total += 1
    pl.semaphore_wait(barrier, total)


def to_peer(axis, distance, source, dest, sems, row):
    return pltpu.make_async_remote_copy(
        src_ref=source,
        dst_ref=dest,
        send_sem=sems.at[0, row, distance - 1],
        recv_sem=sems.at[1, row, distance - 1],
        device_id=axis_peers(axis, distance),
        device_id_type=pl.DeviceIdType.MESH,
    )


def gather_kernel(own_ref, out_ref, sems):
    greet(("shot",))
    me = lax.axis_index("shot")
    copies = [
        to_peer("shot", d, own_ref, out_ref.at[me], sems, 0)
        for d in range(1, lax.axis_size("shot"))
    ]
    for copy in copies:
        copy.start()
    out_ref[me] = own_ref[...]
    for copy in copies:
        copy.wait()


def gather_latent(own):
    shots = lax.axis_size("shot")
    vmem = pl.BlockSpec(memory_space=pltpu.VMEM)
    return pl.pallas_call(
        gather_kernel,
        out_shape=jax.ShapeDtypeStruct((shots,) + own.shape, jnp.float32),
        in_specs=[vmem],
        out_specs=vmem,
        scratch_shapes=[pltpu.SemaphoreType.DMA((2, 1, shots - 1))],
        compiler_params=pltpu.CompilerParams(collective_id=1, has_side_effects=True),
    )(own)


def reduce_kernel(share_ref, weight_ref, out_ref, sum_ref, landed, first, second, third, sems):
    greet(("shot", "gx", "gy"))
    me = lax.axis_index("shot")
    copies = []
    for d in range(1, lax.axis_size("shot")):
        there = axis_peers("shot", d)["shot"]
        copies.append(to_peer("shot", d, weight_ref, first.at[me], sems, 0))
        copies.append(to_peer("shot", d, share_ref.at[there], landed.at[me], sems, 1))
    for copy in copies[::2] + copies[1::2]:
        copy.start()
    first[me] = weight_ref[...]
    landed[me] = share_ref[me]

    def total(stack):
        summed = stack[0]
        for n in range(1, stack.shape[0]):
            summed = summed + stack[n]
        return summed

    for copy in copies[::2]:
        copy.wait()
    held, slots, row = first, second, 2
    for axis in ("gx", "gy"):
        mine = lax.axis_index(axis)
        slots[mine] = total(held)
        hops = [
            to_peer(axis, d, slots.at[mine], slots.at[mine], sems, row)
            for d in range(1, lax.axis_size(axis))
        ]
        for hop in hops:
            hop.start()
        if axis == "gx":
            for copy in copies[1::2]:
                copy.wait()
            out_ref[...] = total(landed)
        for hop in hops:
            hop.wait()
        held, slots, row = slots, third, row + 1
    sum_ref[...] = total(held)


def reduce_all(shares, weights):
    sizes = [lax.axis_size(axis) for axis in ("shot", "gx", "gy")]
    vmem = pl.BlockSpec(memory_space=pltpu.VMEM)
    return pl.pallas_call(
        reduce_kernel,
        out_shape=(
            jax.ShapeDtypeStruct(shares.shape[1:], jnp.float32),
            jax.ShapeDtypeStruct(weights.shape, jnp.float32),
        ),
        in_specs=[vmem, vmem],
        out_specs=(vmem, vmem),
        scratch_shapes=[pltpu.VMEM(shares.shape, jnp.float32)]
        + [pltpu.VMEM((size,) + weights.shape, jnp.float32) for size in sizes]
        + [pltpu.SemaphoreType.DMA((2, 4, max(sizes)))],
        compiler_params=pltpu.CompilerParams(collective_id=2, has_side_effects=True),
    )(shares, weights)


exact = lax.Precision.HIGHEST
contract_lanes = (((1,), (1,)), ((), ()))


def by_offset(values_in):
    offset = lax.broadcasted_iota(jnp.int32, values_in.shape, 1) % 4
    return [jnp.where(offset == k, values_in, 0.0) for k in range(4)]


def decode_kernel(wide_ref, first_ref, second_ref, mod_ref, buoy_ref, hidden_ref, fine_ref):
    rows_b, size_z = wide_ref.shape[1], wide_ref.shape[3]

    def row(a, carry):
        latent = jnp.concatenate([wide_ref[a, b] for b in range(rows_b)], axis=1)
        hidden = jnp.tanh(jnp.dot(first_ref[...], latent, precision=exact))
        hidden_ref[a] = hidden
        fine = jnp.dot(
            second_ref[...], jnp.concatenate(by_offset(hidden), axis=0), precision=exact
        )
        fine_ref[a] = fine
        speed = 0.15 + 0.25 * jax.nn.sigmoid(fine[:16])
        density = 1.0 + 1.5 * jax.nn.sigmoid(fine[16:])
        modulus = density * speed * speed
        buoyancy = 1.0 / density
        for i in range(4):
            for b in range(rows_b):
                lanes = slice(b * size_z, (b + 1) * size_z)
                mod_ref[4 * a + i, 4 * b : 4 * b + 4] = modulus[4 * i : 4 * i + 4, lanes]
                buoy_ref[4 * a + i, 4 * b : 4 * b + 4] = buoyancy[4 * i : 4 * i + 4, lanes]
        return carry

    lax.fori_loop(0, wide_ref.shape[0], row, 0)


def decode(wide, w_first, w_second):
    rows_a, rows_b, channels, size_z = wide.shape
    field = jax.ShapeDtypeStruct((4 * rows_a, 4 * rows_b, size_z), jnp.float32)
    lanes = rows_b * size_z
    by_k = w_second.reshape(channels, 32, 4).transpose(1, 2, 0).reshape(32, 4 * channels)
    return pl.pallas_call(
        decode_kernel,
        out_shape=(
            field,
            field,
            jax.ShapeDtypeStruct((rows_a, channels, lanes), jnp.float32),
            jax.ShapeDtypeStruct((rows_a, 32, lanes), jnp.float32),
        ),
        compiler_params=pltpu.CompilerParams(vmem_limit_bytes=40 * 1024 * 1024),
    )(wide, w_first.T, by_k)


def gradient_kernel(
    totals_ref, wide_ref, hidden_ref, fine_ref, first_ref, back_ref, out_ref, gf_ref, gs_ref, mix
):
    rows_b, size_z = wide_ref.shape[1], wide_ref.shape[3]
    gf_ref[...] = jnp.zeros(gf_ref.shape, jnp.float32)
    gs_ref[...] = jnp.zeros(gs_ref.shape, jnp.float32)

    def row(a, carry):
        for field in range(2):
            for i in range(4):
                for b in range(rows_b):
                    top = 16 * field + 4 * i
                    mix[top : top + 4, b * size_z : (b + 1) * size_z] = totals_ref[
                        field, 4 * a + i, 4 * b : 4 * b + 4
                    ]
        grad_mod, grad_buoy = mix[:16], mix[16:]
        sig_speed = jax.nn.sigmoid(fine_ref[a, :16])
        sig_dens = jax.nn.sigmoid(fine_ref[a, 16:])
        speed = 0.15 + 0.25 * sig_speed
        density = 1.0 + 1.5 * sig_dens
        grad_speed = grad_mod * 2.0 * density * speed
        grad_dens = grad_mod * speed * speed - grad_buoy / (density * density)
        grad_fine = jnp.concatenate(
            [
                grad_speed * 0.25 * sig_speed * (1.0 - sig_speed),
                grad_dens * 1.5 * sig_dens * (1.0 - sig_dens),
            ],
            axis=0,
        )
        hidden = hidden_ref[a]
        channels = hidden.shape[0]
        spread = jnp.dot(back_ref[...], grad_fine, precision=exact)
        offset = lax.broadcasted_iota(jnp.int32, hidden.shape, 1) % 4
        grad_hidden = 0.0
        for k in range(4):
            grad_hidden = grad_hidden + jnp.where(
                offset == k, spread[k * channels : (k + 1) * channels], 0.0
            )
        grad_pre = grad_hidden * (1.0 - hidden * hidden)
        grad_wide = jnp.dot(first_ref[...], grad_pre, precision=exact)
        for b in range(rows_b):
            out_ref[a, b] = grad_wide[:, b * size_z : (b + 1) * size_z]
        latent = jnp.concatenate([wide_ref[a, b] for b in range(rows_b)], axis=1)
        gf_ref[...] += lax.dot_general(
            latent, grad_pre, contract_lanes, precision=exact, preferred_element_type=jnp.float32
        )
        gs_ref[...] += lax.dot_general(
            jnp.concatenate(by_offset(hidden), axis=0),
            grad_fine,
            contract_lanes,
            precision=exact,
            preferred_element_type=jnp.float32,
        )
        return carry

    lax.fori_loop(0, wide_ref.shape[0], row, 0)


def decoder_grads(totals, wide, hidden, fine, w_first, w_second):
    rows_a, rows_b, channels, size_z = wide.shape
    back = w_second.reshape(channels, 32, 4).transpose(2, 0, 1).reshape(4 * channels, 32)
    grad_wide, grad_first, by_k = pl.pallas_call(
        gradient_kernel,
        out_shape=(
            jax.ShapeDtypeStruct(wide.shape, jnp.float32),
            jax.ShapeDtypeStruct((channels, channels), jnp.float32),
            jax.ShapeDtypeStruct((4 * channels, 32), jnp.float32),
        ),
        scratch_shapes=[pltpu.VMEM((32, rows_b * size_z), jnp.float32)],
        compiler_params=pltpu.CompilerParams(vmem_limit_bytes=40 * 1024 * 1024),
    )(totals, wide, hidden, fine, w_first, back)
    grad_second = by_k.reshape(4, channels, 32).transpose(1, 2, 0).reshape(channels, 128)
    return grad_wide, grad_first, grad_second


RIM = 7
VRIM = 4
PAD = 8


def receiver_kernel(column_ref, depth_ref, parts_ref, hits_ref, recorded_ref, weights_ref):
    count = column_ref.shape[1]
    size_x, size_y, size_z = hits_ref.shape
    deep = (
        lax.broadcasted_iota(jnp.int32, (size_z, count), 0) == depth_ref[...]
    ).astype(jnp.float32)
    weights_ref[pl.ds(0, size_z), :] = deep.astype(jnp.bfloat16)
    for part in range(2 * STEPS):
        weights_ref[pl.ds((part + 1) * size_z, size_z), :] = (
            deep * parts_ref[pl.ds(part, 1), :]
        ).astype(jnp.bfloat16)
    chunk = 8 if size_x % 8 == 0 else 1
    rows = chunk * size_y

    def planes(step, carry):
        index = lax.broadcasted_iota(jnp.int32, (rows, count), 0) + step * rows
        picks = (index == column_ref[...]).astype(jnp.float32).astype(jnp.bfloat16)
        summed = lax.dot_general(
            picks, weights_ref[...], (((1,), (1,)), ((), ())), preferred_element_type=jnp.float32
        ).reshape(chunk, size_y, (2 * STEPS + 1) * size_z)
        here = pl.ds(step * chunk, chunk)
        hits_ref[here] = summed[:, :, :size_z]
        for moment in range(STEPS):
            first = (1 + 2 * moment) * size_z
            recorded_ref[moment, here] = (
                summed[:, :, first : first + size_z]
                + summed[:, :, first + size_z : first + 2 * size_z]
            )
        return carry

    lax.fori_loop(0, size_x // chunk, planes, 0)


def receiver_fields(receivers, observed_now, anchor_x, anchor_y, shape):
    size_x, size_y, size_z = shape
    local_x = receivers[0] - anchor_x
    local_y = receivers[1] - anchor_y
    inside = (local_x >= 0) & (local_x < size_x) & (local_y >= 0) & (local_y < size_y)
    column = jnp.where(inside, local_x * size_y + local_y, -1)
    count = column.shape[0]
    high = lax.reduce_precision(observed_now, 8, 7)
    low = lax.reduce_precision(observed_now - high, 8, 7)
    parts = jnp.stack([high, low], axis=1).reshape(2 * STEPS, count)
    return pl.pallas_call(
        receiver_kernel,
        out_shape=(
            jax.ShapeDtypeStruct(shape, jnp.float32),
            jax.ShapeDtypeStruct((STEPS,) + shape, jnp.float32),
        ),
        scratch_shapes=[pltpu.VMEM(((2 * STEPS + 1) * size_z, count), jnp.bfloat16)],
        compiler_params=pltpu.CompilerParams(vmem_limit_bytes=40 * 1024 * 1024),
        cost_estimate=pl.CostEstimate(
            flops=2 * size_x * size_y * count * 7 * size_z,
            bytes_accessed=16 * size_x * size_y * size_z,
            transcendentals=0,
        ),
    )(column[None, :], receivers[2][None, :], parts)


def window_kernel(
    place_ref,
    amp_ref,
    dplus_ref,
    dminus_ref,
    mod_ref,
    buoy_ref,
    fwd_press,
    fwd_vel,
    adj_press,
    adj_vel,
    hits_ref,
    recorded_ref,
    out_ref,
    press,
    buoy,
    vel_x,
    vel_y,
    vel_z,
    diverge_z,
    misfit,
    div_at,
    slope_x,
    slope_y,
    slope_z,
    local_sem,
    send_sem,
    recv_sem,
):
    size_x, size_y, size_z = mod_ref.shape
    tall = size_y + 2 * PAD
    mid_y = pl.ds(PAD, size_y)
    me_x, me_y = lax.axis_index("gx"), lax.axis_index("gy")
    has = (
        me_x > 0,
        me_x < lax.axis_size("gx") - 1,
        me_y > 0,
        me_y < lax.axis_size("gy") - 1,
    )
    target = ({"gx": me_x - 1}, {"gx": me_x + 1}, {"gy": me_y - 1}, {"gy": me_y + 1})

    barrier = pltpu.get_barrier_semaphore()
    for side in range(4):

        @pl.when(has[side])
        def _():
            pl.semaphore_signal(
                barrier, inc=1, device_id=target[side], device_id_type=pl.DeviceIdType.MESH
            )

    loads = [
        (fwd_press, press.at[0, pl.ds(RIM, size_x), mid_y]),
        (buoy_ref, buoy.at[pl.ds(VRIM, size_x), mid_y]),
    ]
    for way, vel in enumerate((fwd_vel, adj_vel)):
        loads.append((vel.at[0], vel_x.at[way, pl.ds(VRIM, size_x)]))
        loads.append((vel.at[1], vel_y.at[way, :, mid_y]))
        loads.append((vel.at[2], vel_z.at[way]))
    moves = [
        pltpu.make_async_copy(source, dest, local_sem.at[n])
        for n, (source, dest) in enumerate(loads)
    ]
    for move in moves:
        move.start()

    def channel(slot, pairs):
        return [
            pltpu.make_async_remote_copy(
                src_ref=pairs[side][0],
                dst_ref=pairs[side][1],
                send_sem=send_sem.at[slot, side],
                recv_sem=recv_sem.at[slot, side ^ 1],
                device_id=target[side],
                device_id_type=pl.DeviceIdType.MESH,
            )
            for side in range(4)
        ]

    def press_pairs(state, edges):
        low_x, high_x = pl.ds(0, RIM), pl.ds(size_x + RIM, RIM)
        low_y, high_y = pl.ds(0, PAD), pl.ds(size_y + PAD, PAD)
        mid_x = pl.ds(RIM, size_x)
        return [
            (edges[0], press.at[state, high_x, mid_y]),
            (edges[1], press.at[state, low_x, mid_y]),
            (edges[2], press.at[state, mid_x, high_y]),
            (edges[3], press.at[state, mid_x, low_y]),
        ]

    def own_edges(state):
        mid_x = pl.ds(RIM, size_x)
        return [
            press.at[state, pl.ds(RIM, RIM), mid_y],
            press.at[state, pl.ds(size_x, RIM), mid_y],
            press.at[state, mid_x, pl.ds(PAD, PAD)],
            press.at[state, mid_x, pl.ds(size_y, PAD)],
        ]

    first_edges = [
        fwd_press.at[pl.ds(0, RIM)],
        fwd_press.at[pl.ds(size_x - RIM, RIM)],
        fwd_press.at[:, pl.ds(0, PAD)],
        fwd_press.at[:, pl.ds(size_y - PAD, PAD)],
    ]
    channels = [channel(0, press_pairs(0, first_edges))]
    for state in range(1, 2 * STEPS):
        channels.append(channel(state, press_pairs(state, own_edges(state))))
    for way, vel in enumerate((fwd_vel, adj_vel)):
        channels.append(
            channel(
                2 * STEPS + way,
                [
                    (vel.at[0, pl.ds(0, VRIM)], vel_x.at[way, pl.ds(size_x + VRIM, VRIM)]),
                    (vel.at[0, pl.ds(size_x - VRIM, VRIM)], vel_x.at[way, pl.ds(0, VRIM)]),
                    (vel.at[1, :, pl.ds(0, PAD)], vel_y.at[way, :, pl.ds(size_y + PAD, PAD)]),
                    (vel.at[1, :, pl.ds(size_y - PAD, PAD)], vel_y.at[way, :, pl.ds(0, PAD)]),
                ],
            )
        )
    mid_v = pl.ds(VRIM, size_x)
    channels.append(
        channel(
            2 * STEPS + 2,
            [
                (buoy_ref.at[pl.ds(0, VRIM)], buoy.at[pl.ds(size_x + VRIM, VRIM), mid_y]),
                (buoy_ref.at[pl.ds(size_x - VRIM, VRIM)], buoy.at[pl.ds(0, VRIM), mid_y]),
                (buoy_ref.at[:, pl.ds(0, PAD)], buoy.at[mid_v, pl.ds(size_y + PAD, PAD)]),
                (buoy_ref.at[:, pl.ds(size_y - PAD, PAD)], buoy.at[mid_v, pl.ds(0, PAD)]),
            ],
        )
    )

    def send(slot, sides):
        for side in sides:

            @pl.when(has[side])
            def _():
                channels[slot][side].start()

    def receive(slot):
        for side in range(4):

            @pl.when(has[side])
            def _():
                channels[slot][side ^ 1].wait_recv()

    def sent(slot):
        for side in range(4):

            @pl.when(has[side])
            def _():
                channels[slot][side].wait_send()

    for side in range(4):

        @pl.when(jnp.logical_not(has[side]))
        def _():
            far = side % 2
            if side < 2:
                rows = pl.ds(far * (size_x + RIM), RIM)
                vrows = pl.ds(far * (size_x + VRIM), VRIM)
                for state in range(2 * STEPS):
                    press[state, rows, mid_y] = jnp.zeros((RIM, size_y, size_z), jnp.float32)
                buoy[vrows, mid_y] = jnp.zeros((VRIM, size_y, size_z), jnp.float32)
                for way in range(2):
                    vel_x[way, vrows] = jnp.zeros((VRIM, size_y, size_z), jnp.float32)
            else:
                cols = pl.ds(far * (size_y + PAD), PAD)
                blank = jnp.zeros((size_x, PAD, size_z), jnp.float32)
                for state in range(2 * STEPS):
                    press[state, pl.ds(RIM, size_x), cols] = blank
                buoy[mid_v, cols] = blank
                for way in range(2):
                    vel_y[way, :, cols] = blank

    peers = sum(jnp.where(here, 1, 0) for here in has)
    pl.semaphore_wait(barrier, peers)

    every = range(4)
    send(0, every)
    send(2 * STEPS + 2, every)
    send(2 * STEPS, every)
    send(2 * STEPS + 1, every)
    for move in moves:
        move.wait()

    src_x, src_y, src_z = place_ref[0], place_ref[1], place_ref[2]
    at_source = (
        (lax.broadcasted_iota(jnp.int32, (size_y, size_z), 0) == src_y)
        & (lax.broadcasted_iota(jnp.int32, (size_y, size_z), 1) == src_z)
    ).astype(jnp.float32)
    chunk = 8 if size_x % 8 == 0 else 1
    def step(state, way, moment):
        def depth_part(turn, carry):
            here = pl.ds(turn * chunk, chunk)
            inner = press[state, pl.ds(turn * chunk + RIM, chunk), mid_y]
            slope = jnp.dot(
                inner.reshape(chunk * size_y, size_z), dplus_ref[...], precision=exact
            ).reshape(inner.shape)
            if way == 0:
                slope_z[moment, here] = slope
            moved = vel_z[way, here] - buoy_ref_in(turn) * slope
            vel_z[way, here] = moved
            diverge_z[here] = jnp.dot(
                moved.reshape(chunk * size_y, size_z), dminus_ref[...], precision=exact
            ).reshape(inner.shape)
            return carry

        def buoy_ref_in(turn):
            return buoy[pl.ds(turn * chunk + VRIM, chunk), mid_y]

        lax.fori_loop(0, size_x // chunk, depth_part, 0)

        if state == 0:
            receive(2 * STEPS + 2)
        if state % STEPS == 0:
            receive(2 * STEPS + way)
        receive(state)

        def along_x(i):
            slope = 0.0
            for order, weight in enumerate(coeffs):
                r = order + 1
                slope = slope + weight * (
                    press[state, i + VRIM - 1 + r, mid_y] - press[state, i + VRIM - r, mid_y]
                )
            vel_x[way, i] = vel_x[way, i] - buoy[i, mid_y] * slope
            return slope

        def ghost_low(i, carry):
            along_x(i)
            return carry

        def faces(x, carry):
            slope = along_x(x + VRIM)
            plane = press[state, x + RIM]
            slope_b = 0.0
            for order, weight in enumerate(coeffs):
                r = order + 1
                back = plane if r == 1 else pltpu.roll(plane, r - 1, 0)
                slope_b = slope_b + weight * (pltpu.roll(plane, tall - r, 0) - back)
            vel_y[way, x] = vel_y[way, x] - buoy[x + VRIM] * slope_b
            if way == 0:
                slope_x[moment, x] = slope
                slope_y[moment, x] = slope_b[PAD : PAD + size_y]
            return carry

        lax.fori_loop(0, VRIM, ghost_low, 0)
        lax.fori_loop(size_x + VRIM, size_x + 2 * VRIM - 1, ghost_low, 0)
        lax.fori_loop(0, size_x, faces, 0, unroll=2)

        def finish(k, carry):
            x = lax.rem(k + size_x - RIM, size_x)
            plane = vel_y[way, x]
            div = diverge_z[x]
            across = 0.0
            for order, weight in enumerate(coeffs):
                r = order + 1
                ahead = plane if r == 1 else pltpu.roll(plane, tall - r + 1, 0)
                across = across + weight * (ahead - pltpu.roll(plane, r, 0))
                div = div + weight * (
                    vel_x[way, x + VRIM + r - 1] - vel_x[way, x + VRIM - r]
                )
            div = div + across[PAD : PAD + size_y]
            value = press[state, x + RIM, mid_y] - mod_ref[x] * div
            if way == 0:
                value = value + at_source * jnp.where(x == src_x, amp_ref[moment], 0.0)
                residue = hits_ref[x] * value - recorded_ref[moment, x]
                div_at[moment, x] = div
                if moment == STEPS - 1:
                    press[state + 1, x + RIM, mid_y] = adj_press[x] + residue
                else:
                    misfit[moment, x] = residue
                    press[state + 1, x + RIM, mid_y] = value
            else:
                part_mod = value * div_at[moment, x]
                part_buoy = (
                    vel_x[way, x + VRIM] * slope_x[moment, x]
                    + plane[PAD : PAD + size_y] * slope_y[moment, x]
                    + vel_z[way, x] * slope_z[moment, x]
                )
                if moment == STEPS - 1:
                    out_ref[0, x] = -part_mod
                    out_ref[1, x] = -part_buoy
                else:
                    out_ref[0, x] = out_ref[0, x] - part_mod
                    out_ref[1, x] = out_ref[1, x] - part_buoy
                if moment > 0:
                    press[state + 1, x + RIM, mid_y] = value + misfit[moment - 1, x]
            return carry

        edge = min(2 * RIM, size_x)
        lax.fori_loop(0, edge, finish, 0, unroll=2)
        more = state + 1 < 2 * STEPS
        if more:
            send(state + 1, (0, 1))
        lax.fori_loop(edge, size_x, finish, 0, unroll=2)
        if more:
            send(state + 1, (2, 3))

    for moment in range(STEPS):
        step(moment, 0, moment)
    for turn in range(STEPS):
        step(STEPS + turn, 1, STEPS - 1 - turn)
    for slot in range(2 * STEPS + 3):
        sent(slot)


def depth_matrices(size_z):
    source = lax.broadcasted_iota(jnp.int32, (size_z, size_z), 0)
    dest = lax.broadcasted_iota(jnp.int32, (size_z, size_z), 1)
    plus = jnp.zeros((size_z, size_z), jnp.float32)
    minus = plus
    for order, weight in enumerate(coeffs):
        r = order + 1
        plus = plus + jnp.where(source == dest + r, weight, 0.0)
        plus = plus - jnp.where(source == dest - r + 1, weight, 0.0)
        minus = minus + jnp.where(source == dest + r - 1, weight, 0.0)
        minus = minus - jnp.where(source == dest - r, weight, 0.0)
    return plus, minus


def window(place, amps, modulus, buoyancy, fwd_press, fwd_vel, adj_press, adj_vel, hits, recorded):
    size_x, size_y, size_z = fwd_press.shape
    tall = size_y + 2 * PAD
    plus, minus = depth_matrices(size_z)
    vmem = pl.BlockSpec(memory_space=pltpu.VMEM)
    smem = pl.BlockSpec(memory_space=pltpu.SMEM)
    field = (size_x, size_y, size_z)

    def scratch(*shape):
        return pltpu.VMEM(shape, jnp.float32)

    slots = 2 * STEPS + 3
    return pl.pallas_call(
        window_kernel,
        out_shape=jax.ShapeDtypeStruct((2,) + field, jnp.float32),
        in_specs=[smem, smem] + [vmem] * 10,
        out_specs=vmem,
        scratch_shapes=[
            scratch(2 * STEPS, size_x + 2 * RIM, tall, size_z),
            scratch(size_x + 2 * VRIM, tall, size_z),
            scratch(2, size_x + 2 * VRIM, size_y, size_z),
            scratch(2, size_x, tall, size_z),
            scratch(2, *field),
            scratch(*field),
            scratch(STEPS - 1, *field),
            scratch(STEPS, *field),
            scratch(STEPS, *field),
            scratch(STEPS, *field),
            scratch(STEPS, *field),
            pltpu.SemaphoreType.DMA((8,)),
            pltpu.SemaphoreType.DMA((slots, 4)),
            pltpu.SemaphoreType.DMA((slots, 4)),
        ],
        compiler_params=pltpu.CompilerParams(
            collective_id=0, has_side_effects=True, vmem_limit_bytes=56 * 1024 * 1024
        ),
    )(place, amps, plus, minus, modulus, buoyancy, fwd_press, fwd_vel, adj_press, adj_vel, hits, recorded)


def body(
    latent,
    w_first,
    w_second,
    fwd_press,
    fwd_vel,
    adj_press,
    adj_vel,
    src_pos,
    src_amp,
    rec_pos,
    observed,
):
    size_x, size_y = (fwd_press.shape[1], fwd_press.shape[2])
    anchor_x = lax.axis_index("gx") * size_x
    anchor_y = lax.axis_index("gy") * size_y
    depth_c, rows_x, merged = latent.shape
    size_z = fwd_press.shape[3]
    everything = gather_latent(latent.reshape(depth_c, rows_x * merged))
    all_depth = size_z // 4
    repeat = (
        lax.broadcasted_iota(jnp.int32, (all_depth, size_z), 1) // 4
        == lax.broadcasted_iota(jnp.int32, (all_depth, size_z), 0)
    ).astype(jnp.float32)
    wide = lax.dot_general(
        everything.reshape(all_depth, rows_x * merged),
        repeat,
        (((0,), (0,)), ((), ())),
        precision=exact,
    ).reshape(rows_x, merged // CH, CH, size_z)
    modulus, buoyancy, hidden, fine = decode(wide, w_first, w_second)
    hits, recorded = receiver_fields(
        rec_pos[0], observed[0], anchor_x, anchor_y, fwd_press.shape[1:]
    )
    place = jnp.stack([src_pos[0, 0] - anchor_x, src_pos[1, 0] - anchor_y, src_pos[2, 0]])
    totals = window(
        place,
        src_amp[:, 0],
        modulus,
        buoyancy,
        fwd_press[0],
        fwd_vel[0],
        adj_press[0],
        adj_vel[0],
        hits,
        recorded,
    )
    grad_wide, grad_first, grad_second = decoder_grads(
        totals, wide, hidden, fine, w_first, w_second
    )
    grad_depth = lax.dot_general(
        repeat, grad_wide.reshape(rows_x * merged, size_z), contract_lanes, precision=exact
    )
    weights = jnp.concatenate(
        [grad_second, jnp.pad(grad_first, ((0, 0), (0, 128 - CH)))], axis=0
    )
    own, weights = reduce_all(grad_depth.reshape(-1, depth_c, rows_x * merged), weights)
    return (own.reshape(latent.shape), weights[CH:, :CH], weights[:CH])


def solution(mesh):
    in_specs = (
        P("shot", "gx", "gy"),
        P(),
        P(),
        P("shot", "gx", "gy", None),
        P("shot", None, "gx", "gy", None),
        P("shot", "gx", "gy", None),
        P("shot", None, "gx", "gy", None),
        P(None, "shot"),
        P(None, "shot"),
        P("shot", None, None),
        P("shot", None, None),
    )
    out_specs = (P("shot", "gx", "gy"), P(), P())
    return jax.shard_map(body, mesh=mesh, in_specs=in_specs, out_specs=out_specs, check_vma=False)
```

profile of v0, /device:TPU:0, one launch (start us, length us, event | category | flops | bytes accessed | tf_op | source)
XLA Modules:
  0.0 120.5 jit_solution(11928300076057921796)
XLA Ops:
  0.6 0.8 slice_bitcast_fusion
  1.4 0.8 bitcast_reduce-precision_fusion
  2.2 0.1 pad_maximum_fusion
  2.3 4.3 %shard_map.132 = (f32[24,32,128]{2,1,0:T(8,128)S(1)}, f32[3,24,32,128]{3,2,1,0:T(8,128)S(1)}) custom-call(s32[1,2048]{1,0:T(1,128)S(1)} %get-tuple-element.28.column_ref, s32[1,2048]{1,0:T(1,128)S(1)} %get-tuple-element.27.depth_ref, f32[6,2048]{1,0:T(8,128)S(1)} %reshape.174.parts_ref), custom_call_target="tpu_custom_call" | custom-call | flops 2818572288 | bytes 1572864 | tf_op jit(solution)/shard_map/pallas_call | solution.py:306
  6.6 0.0 copy-start.3
  6.6 1.0 copy-done.3
  7.6 0.0 copy-start.6
  7.6 0.8 copy-done.6
  8.4 9.4 %shard_map.130 = f32[4,8,3072]{2,1,0:T(8,128)} custom-call(f32[8,3072]{1,0:T(8,128)} %bitcast.58), custom_call_target="tpu_custom_call" | custom-call | tf_op jit(solution)/shard_map/pallas_call | solution.py:63
  17.8 1.8 %convolution_bitcast_fusion = f32[3072,128]{0,1:T(8,128)S(1)} fusion(f32[4,8,3072]{2,1,0:T(8,128)} %shard_map.130, s32[128]{0:T(128)S(1)} %get-tuple-element.42, s32[128]{0:T(128)S(1)} %get-tuple-element.43, pred[128]{0:T(512)(128)(4,1)S(1)} %compare_and_fusion), kind=kOutput, calls=%fused_computation | convolution fusion | flops 151003136 | bytes 1967232 | tf_op jit(solution)/shard_map/dot_general | solution.py:707
  19.7 0.0 copy-start.10
  19.7 0.0 copy-start.9
  19.7 0.5 copy.19
  20.1 0.0 copy-start.11
  20.2 0.3 copy-done.10
  20.4 0.1 copy.21
  20.5 0.1 reshape.173.second_ref
  20.6 0.0 copy-done.9
  20.6 0.1 copy.20
  20.7 5.9 %shard_map.131 = (f32[24,32,128]{2,1,0:T(8,128)S(1)}, f32[24,32,128]{2,1,0:T(8,128)S(1)}, f32[6,64,1024]{2,1,0:T(8,128)S(1)}, f32[6,32,1024]{2,1,0:T(8,128)S(1)}) custom-call(f32[6,8,64,128]{3,2,1,0:T(8,128)S(1)} %bitcast.44, f32[64,64]{1,0:T(8,128)S(1)} %bitcast.48, f32[32,256]{1,0:T(8,128)S(1)} %reshape.173.second_ref), custom_call_target="tpu_custom_call" | custom-call | tf_op jit(solution)/shard_map/pallas_call | solution.py:171
  26.6 0.0 copy-start.1
  26.6 1.1 copy-done.1
  27.7 0.0 copy-start.4
  27.7 0.9 copy-done.4
  28.6 0.0 copy-start.7
  28.6 0.8 copy-done.7
  29.4 0.0 copy-start.8
  29.4 0.8 copy-done.8
  30.2 0.0 copy-done.11
  30.2 0.6 fusion.35
  32.0 1.2 %pad_add_fusion.place_ref = s32[3]{0:T(128)} fusion(s32[1]{0:T(128)} %bitcast.4, s32[1]{0:T(128)} %bitcast.3, s32[1]{0:T(128)} %bitcast.1), kind=kLoop, calls=%fused_computation.68 | loop fusion | flops 6 | bytes 24 | tf_op jit(solution)/shard_map/stack | solution.py:717
  33.3 0.7 fusion.16
  34.0 45.2 %shard_map.133.totals_ref = f32[2,24,32,128]{3,2,1,0:T(8,128)} custom-call(s32[3]{0:T(128)} %pad_add_fusion.place_ref, f32[3]{0:T(128)} %bitcast.59, f32[128,128]{1,0:T(8,128)} %get-tuple-element.30.dplus_ref, f32[128,128]{1,0:T(8,128)} %get-tuple-element.29.dminus_ref, f32[24,32,128]{2,1,0:T(8,128)} %copy-done.7, f32[24,32,128]{2,1,0:T(8,128)} %copy-done.8, ...), custom_call_target="tpu_custom_call" | custom-call | tf_op jit(solution)/shard_map/pallas_call | solution.py:656
  79.2 0.1 copy.22
  79.3 0.0 copy-start
  79.3 1.1 copy-done
  80.4 0.0 copy-start.2
  80.5 1.4 %copy-done.2 = f32[6,64,1024]{2,1,0:T(8,128)S(1)} copy-done((f32[6,64,1024]{2,1,0:T(8,128)S(1)}, f32[6,64,1024]{2,1,0:T(8,128)}, u32[]{:S(2)}) %copy-start.2) | copy-done | bytes 1572888
  81.9 0.0 copy-start.5
  81.9 1.1 copy-done.5
  83.0 13.8 %shard_map.134 = (f32[6,8,64,128]{3,2,1,0:T(8,128)S(1)}, f32[64,64]{1,0:T(8,128)S(1)}, f32[256,32]{1,0:T(8,128)S(1)}) custom-call(f32[2,24,32,128]{3,2,1,0:T(8,128)S(1)} %copy-done, f32[6,8,64,128]{3,2,1,0:T(8,128)S(1)} %bitcast.45, f32[6,64,1024]{2,1,0:T(8,128)S(1)} %copy-done.2, f32[6,32,1024]{2,1,0:T(8,128)S(1)} %copy-done.5, f32[64,64]{1,0:T(8,128)S(1)} %copy-done.9, ...), custom_call_target="tpu_custom_call" | custom-call | tf_op jit(solution)/shard_map/pallas_call | solution.py:244
  96.8 0.1 copy.23
  96.9 0.1 copy.24
  97.0 0.7 select_maximum_fusion.weight_ref
  97.6 1.7 %fusion.26.share_ref = f32[4,8,3072]{2,1,0:T(8,128)} fusion(f32[3072,128,1]{1,0,2:T(8,128)S(1)} %bitcast.46, s32[4,8]{1,0:T(4,128)S(1)} %multiply_add_fusion, s32[128]{0:T(128)S(1)} %get-tuple-element.42, s32[128]{0:T(128)S(1)} %get-tuple-element.43, pred[128]{0:T(512)(128)(4,1)S(1)} %compare_and_fusion), kind=kOutput, calls=%fused_computation.46 | convolution fusion | flops 151003136 | bytes 1967360 | tf_op jit(solution)/shard_map/dot_general | solution.py:733
  99.4 16.8 %shard_map.135 = (f32[8,3072]{1,0:T(8,128)}, f32[128,128]{1,0:T(8,128)}) custom-call(f32[4,8,3072]{2,1,0:T(8,128)} %fusion.26.share_ref, f32[128,128]{1,0:T(8,128)} %select_maximum_fusion.weight_ref), custom_call_target="tpu_custom_call" | custom-call | tf_op jit(solution)/shard_map/pallas_call | solution.py:117
  116.2 1.4 %slice.36 = f32[64,64]{1,0:T(8,128)} slice(f32[128,128]{1,0:T(8,128)} %get-tuple-element.24), slice={[64:128], [0:64]} | slice | bytes 32768 | tf_op jit(solution)/shard_map/slice | solution.py:740
  117.6 1.4 %slice.37 = f32[64,128]{1,0:T(8,128)} slice(f32[128,128]{1,0:T(8,128)} %get-tuple-element.24), slice={[0:64], [0:128]} | slice | bytes 65536 | tf_op jit(solution)/shard_map/slice | solution.py:740
  119.0 1.5 %copy.26 = f32[8,6,512]{2,0,1:T(8,128)} copy(f32[8,6,512]{2,0,1:T(8,128)} %bitcast.57) | data formatting | bytes 196608
  (8 shorter events, 0.1 us)
Async XLA Ops:
  6.6 1.0 copy-start.3
  7.6 0.8 copy-start.6
  19.7 0.8 copy-start.10
  19.7 1.0 copy-start.9
  20.1 10.0 %copy-start.11 = (s32[3,1]{0,1:T(1,128)S(1)}, s32[3,1]{0,1:T(1,128)}, u32[]{:S(2)}) copy-start(s32[3,1]{0,1:T(1,128)} %param.18) | copy-start | bytes 40
  26.6 1.2 copy-start.1
  27.7 0.9 copy-start.4
  28.6 0.8 copy-start.7
  29.4 0.8 copy-start.8
  79.3 1.1 copy-start
  80.4 1.4 %copy-start.2 = (f32[6,64,1024]{2,1,0:T(8,128)S(1)}, f32[6,64,1024]{2,1,0:T(8,128)}, u32[]{:S(2)}) copy-start(f32[6,64,1024]{2,1,0:T(8,128)} %copy-done.1) | copy-start | bytes 4718596
  81.9 1.1 copy-start.5
where the time goes:
time: 121 us
  Pallas kernels  95.4 us (79%)
  local copies, waits for them, and re-layouts  15.2 us (13%)
  other arithmetic  4.25 us (4%)
  matrix products  3.55 us (3%)
  between operations  2.11 us (2%)
    pallas_call x1, Pallas kernels, window(): pl.pallas_call(window_kernel, out_shape=jax.ShapeDtypeStruct((2,) + field...  45.2 us
    pallas_call x1, Pallas kernels, reduce_all(): pl.pallas_call(reduce_kernel, out_shape=(jax.ShapeDtypeStruct(shares.shap...  16.8 us
    pallas_call x1, Pallas kernels, decoder_grads(): pl.pallas_call(gradient_kernel, out_shape=(jax.ShapeDtypeStruct(wide.shap...  13.8 us
    unnamed x27, local copies, waits for them, and re-layouts  11 us
    pallas_call x1, Pallas kernels, gather_latent(): pl.pallas_call(gather_kernel, out_shape=jax.ShapeDtypeStruct((shots,) + o...  9.44 us
    pallas_call x1, Pallas kernels, decode(): pl.pallas_call(decode_kernel, out_shape=(field, field, jax.ShapeDtypeStru...  5.86 us
    pallas_call x1, Pallas kernels, receiver_fields(): pl.pallas_call(receiver_kernel, out_shape=(jax.ShapeDtypeStruct(shape, jn...  4.3 us
    slice x2, local copies, waits for them, and re-layouts, body(): return (own.reshape(latent.shape), weights[CH:, :CH], weights[:CH])  2.75 us

commit v1 on v0

v1 whole, which is shorter than its diff:
```python
import jax
import jax.numpy as jnp
from jax import lax
from jax.experimental import pallas as pl
from jax.experimental.pallas import tpu as pltpu
from jax.sharding import PartitionSpec as P

CH = 64
STEPS = 3
RIM = 7
VRIM = 4
PAD = 8
GROUP = 4
LANES = 128

coeffs = (1225.0 / 1024.0, -245.0 / 3072.0, 49.0 / 5120.0, -5.0 / 7168.0)

rows_by_cols = (((1,), (0,)), ((), ()))
rows_by_rows = (((1,), (1,)), ((), ()))
half = jnp.bfloat16


def split(values):
    high = values.astype(half)
    return high, (values - high.astype(jnp.float32)).astype(half)


def mm(left, right, how=rows_by_cols):
    return lax.dot_general(left, right, how, preferred_element_type=jnp.float32)


def mm3(left, right, how=rows_by_cols):
    return (
        mm(left[0], right[0], how) + mm(left[1], right[0], how) + mm(left[0], right[1], how)
    )


def mm2(left, pick, how=rows_by_cols):
    return mm(left[0], pick, how) + mm(left[1], pick, how)


def one_hot(shape, rule):
    rows = lax.broadcasted_iota(jnp.int32, shape, 0)
    cols = lax.broadcasted_iota(jnp.int32, shape, 1)
    return rule(rows, cols)


def as_pick(mask):
    return jnp.where(mask, 1.0, 0.0).astype(half)


def axis_peers(axis, distance):
    count = lax.axis_size(axis)
    return {axis: lax.rem(lax.axis_index(axis) + distance, count)}


def plane_peers():
    near, wide = lax.axis_size("gy"), lax.axis_size("gx")
    for dx in range(wide):
        for dy in range(near):
            if dx or dy:
                yield {
                    "gx": lax.rem(lax.axis_index("gx") + dx, wide),
                    "gy": lax.rem(lax.axis_index("gy") + dy, near),
                }


def everyone():
    for d in range(1, lax.axis_size("shot")):
        yield axis_peers("shot", d)
    yield from plane_peers()


def remote(source, dest, send_sem, recv_sem, peer):
    return pltpu.make_async_remote_copy(
        src_ref=source,
        dst_ref=dest,
        send_sem=send_sem,
        recv_sem=recv_sem,
        device_id=peer,
        device_id_type=pl.DeviceIdType.MESH,
    )


def logistic(values):
    return 0.5 * jnp.tanh(0.5 * values) + 0.5


def whole_kernel(
    latent_ref,
    first_ref,
    second_ref,
    fwd_press,
    fwd_vel,
    adj_press,
    adj_vel,
    src_pos,
    src_amp,
    rec_pos,
    observed,
    own_ref,
    sums_ref,
    w_first,
    w_second,
    place,
    amps,
    rec_at,
    seen,
    start_adj,
    slabs,
    latents,
    hidden,
    gates,
    hits,
    recorded,
    rec_weights,
    mod,
    press,
    buoy,
    vel_x,
    vel_y,
    vel_z,
    diverge_z,
    misfit,
    div_at,
    slope_x,
    slope_y,
    slope_z,
    totals,
    turned,
    share,
    landed,
    w_share,
    w_landed,
    w_plane,
    local_sem,
    send_sem,
    recv_sem,
    shot_send,
    shot_recv,
    plane_send,
    plane_recv,
):
    size_x, size_y, size_z = mod.shape
    cells = size_z // 4
    tall = size_y + 2 * PAD
    mid_y = pl.ds(PAD, size_y)
    mid_v = pl.ds(VRIM, size_x)
    rows_a = size_x // 4
    wide = GROUP * CH
    halves = size_y // (4 * GROUP)
    shots = lax.axis_size("shot")
    me = lax.axis_index("shot")
    me_x, me_y = lax.axis_index("gx"), lax.axis_index("gy")
    has = (
        me_x > 0,
        me_x < lax.axis_size("gx") - 1,
        me_y > 0,
        me_y < lax.axis_size("gy") - 1,
    )
    target = ({"gx": me_x - 1}, {"gx": me_x + 1}, {"gy": me_y - 1}, {"gy": me_y + 1})

    barrier = pltpu.get_barrier_semaphore()
    greeted = 0
    for peer in everyone():
        pl.semaphore_signal(
            barrier, inc=1, device_id=peer, device_id_type=pl.DeviceIdType.MESH
        )
        greeted += 1

    loads = [
        (first_ref, w_first),
        (second_ref, w_second),
        (rec_pos, rec_at),
        (observed, seen),
        (src_pos, place),
        (src_amp, amps),
        (latent_ref, slabs.at[me]),
        (fwd_press, press.at[0, pl.ds(RIM, size_x), mid_y]),
        (adj_press, start_adj),
    ]
    for way, vel in enumerate((fwd_vel, adj_vel)):
        loads.append((vel.at[0], vel_x.at[way, pl.ds(VRIM, size_x)]))
        loads.append((vel.at[1], vel_y.at[way, :, mid_y]))
        loads.append((vel.at[2], vel_z.at[way]))
    moves = [
        pltpu.make_async_copy(source, dest, local_sem.at[n])
        for n, (source, dest) in enumerate(loads)
    ]
    for move in moves:
        move.start()

    def channel(slot, pairs):
        return [
            remote(
                pairs[side][0],
                pairs[side][1],
                send_sem.at[slot, side],
                recv_sem.at[slot, side ^ 1],
                target[side],
            )
            for side in range(4)
        ]

    def press_pairs(state, edges):
        low_x, high_x = pl.ds(0, RIM), pl.ds(size_x + RIM, RIM)
        low_y, high_y = pl.ds(0, PAD), pl.ds(size_y + PAD, PAD)
        mid_x = pl.ds(RIM, size_x)
        return [
            (edges[0], press.at[state, high_x, mid_y]),
            (edges[1], press.at[state, low_x, mid_y]),
            (edges[2], press.at[state, mid_x, high_y]),
            (edges[3], press.at[state, mid_x, low_y]),
        ]

    def own_edges(state):
        mid_x = pl.ds(RIM, size_x)
        return [
            press.at[state, pl.ds(RIM, RIM), mid_y],
            press.at[state, pl.ds(size_x, RIM), mid_y],
            press.at[state, mid_x, pl.ds(PAD, PAD)],
            press.at[state, mid_x, pl.ds(size_y, PAD)],
        ]

    first_edges = [
        fwd_press.at[pl.ds(0, RIM)],
        fwd_press.at[pl.ds(size_x - RIM, RIM)],
        fwd_press.at[:, pl.ds(0, PAD)],
        fwd_press.at[:, pl.ds(size_y - PAD, PAD)],
    ]
    channels = [channel(0, press_pairs(0, first_edges))]
    for state in range(1, 2 * STEPS):
        channels.append(channel(state, press_pairs(state, own_edges(state))))
    for way, vel in enumerate((fwd_vel, adj_vel)):
        channels.append(
            channel(
                2 * STEPS + way,
                [
                    (vel.at[0, pl.ds(0, VRIM)], vel_x.at[way, pl.ds(size_x + VRIM, VRIM)]),
                    (vel.at[0, pl.ds(size_x - VRIM, VRIM)], vel_x.at[way, pl.ds(0, VRIM)]),
                    (vel.at[1, :, pl.ds(0, PAD)], vel_y.at[way, :, pl.ds(size_y + PAD, PAD)]),
                    (vel.at[1, :, pl.ds(size_y - PAD, PAD)], vel_y.at[way, :, pl.ds(0, PAD)]),
                ],
            )
        )
    channels.append(
        channel(
            2 * STEPS + 2,
            [
                (buoy.at[pl.ds(VRIM, VRIM), mid_y], buoy.at[pl.ds(size_x + VRIM, VRIM), mid_y]),
                (buoy.at[pl.ds(size_x, VRIM), mid_y], buoy.at[pl.ds(0, VRIM), mid_y]),
                (buoy.at[mid_v, pl.ds(PAD, PAD)], buoy.at[mid_v, pl.ds(size_y + PAD, PAD)]),
                (buoy.at[mid_v, pl.ds(size_y, PAD)], buoy.at[mid_v, pl.ds(0, PAD)]),
            ],
        )
    )

    def send(slot, sides):
        for side in sides:

            @pl.when(has[side])
            def _():
                channels[slot][side].start()

    def receive(slot):
        for side in range(4):

            @pl.when(has[side])
            def _():
                channels[slot][side ^ 1].wait_recv()

    def sent(slot):
        for side in range(4):

            @pl.when(has[side])
            def _():
                channels[slot][side].wait_send()

    for side in range(4):

        @pl.when(jnp.logical_not(has[side]))
        def _():
            far = side % 2
            if side < 2:
                rows = pl.ds(far * (size_x + RIM), RIM)
                vrows = pl.ds(far * (size_x + VRIM), VRIM)
                for state in range(2 * STEPS):
                    press[state, rows, mid_y] = jnp.zeros((RIM, size_y, size_z), jnp.float32)
                buoy[vrows, mid_y] = jnp.zeros((VRIM, size_y, size_z), jnp.float32)
                for way in range(2):
                    vel_x[way, vrows] = jnp.zeros((VRIM, size_y, size_z), jnp.float32)
            else:
                cols = pl.ds(far * (size_y + PAD), PAD)
                blank = jnp.zeros((size_x, PAD, size_z), jnp.float32)
                for state in range(2 * STEPS):
                    press[state, pl.ds(RIM, size_x), cols] = blank
                buoy[mid_v, cols] = blank
                for way in range(2):
                    vel_y[way, :, cols] = blank

    pl.semaphore_wait(barrier, greeted)

    gathers = [
        remote(
            latent_ref,
            slabs.at[me],
            shot_send.at[0, d - 1],
            shot_recv.at[0, d - 1],
            axis_peers("shot", d),
        )
        for d in range(1, shots)
    ]
    for copy in gathers:
        copy.start()
    every = range(4)
    send(0, every)
    send(2 * STEPS, every)
    send(2 * STEPS + 1, every)
    for move in moves:
        move.wait()

    spread_rows = as_pick(one_hot((wide, CH), lambda r, c: r % CH == c))
    same_cell = one_hot((wide, wide), lambda r, c: r // CH == c // CH)
    big_first = tuple(
        jnp.where(same_cell, mm(mm(spread_rows, part).astype(half), spread_rows, rows_by_rows), 0.0)
        .astype(half)
        for part in split(w_first[...])
    )
    outs = w_second.shape[1]
    block = outs // 4 * GROUP

    def source_of(c):
        return c % block // 64 * 64 + c % 64 // 16 * 16 + c % 4 * 4 + c // block

    order = as_pick(one_hot((outs, 4 * block), lambda r, c: source_of(c) == r))
    same_out = one_hot((wide, 4 * block), lambda r, c: c % 16 // 4 == r // CH)
    big_second = tuple(
        jnp.where(same_out, mm(mm(spread_rows, part).astype(half), order), 0.0).astype(half)
        for part in split(w_second[...])
    )
    depth_pick = as_pick(one_hot((size_z, size_z), lambda r, c: 4 * (r % cells) + r // cells == c))

    count = rec_at.shape[1]
    local_x = rec_at[0:1] - me_x * size_x
    local_y = rec_at[1:2] - me_y * size_y
    inside = (local_x >= 0) & (local_x < size_x) & (local_y >= 0) & (local_y < size_y)
    column = jnp.where(inside, local_x * size_y + local_y, -1)
    deep = jnp.where(
        lax.broadcasted_iota(jnp.int32, (size_z, count), 0) == rec_at[2:3], 1.0, 0.0
    )
    rec_weights[pl.ds(0, size_z)] = deep.astype(half)
    for moment in range(STEPS):
        for part, values in enumerate(split(seen[moment : moment + 1])):
            rec_weights[pl.ds((1 + 2 * moment + part) * size_z, size_z)] = (
                deep * values.astype(jnp.float32)
            ).astype(half)
    chunk = 8 if size_x % 8 == 0 else 1
    some = chunk * size_y

    def planes(step, carry):
        index = lax.broadcasted_iota(jnp.int32, (some, count), 0) + step * some
        summed = mm(as_pick(index == column), rec_weights[...], rows_by_rows).reshape(
            chunk, size_y, (2 * STEPS + 1) * size_z
        )
        here = pl.ds(step * chunk, chunk)
        hits[here] = summed[:, :, :size_z]
        for moment in range(STEPS):
            first = (1 + 2 * moment) * size_z
            recorded[moment, here] = (
                summed[:, :, first : first + size_z]
                + summed[:, :, first + size_z : first + 2 * size_z]
            )
        return carry

    lax.fori_loop(0, size_x // chunk, planes, 0)

    for copy in gathers:
        copy.wait()
    depth_c = slabs.shape[1]
    for s in range(shots):
        slab = jnp.transpose(slabs[s], (1, 0, 2))
        for a in range(rows_a):
            latents[pl.ds(a * cells + s * depth_c, depth_c)] = slab[a]
    for h in range(halves):
        lanes = slice(h * wide, (h + 1) * wide)
        state = jnp.tanh(mm3(split(latents[:, lanes]), big_first))
        hidden[:, lanes] = state
        outputs = mm3(split(state), big_second)
        for a in range(rows_a):
            rows = slice(a * cells, (a + 1) * cells)
            stacked = jnp.concatenate(
                [outputs[rows, k * block : (k + 1) * block] for k in range(4)], axis=0
            )
            sig = logistic(mm2(split(jnp.transpose(stacked)), depth_pick))
            gates[h, a] = sig
            speed = 0.15 + 0.25 * sig[: block // 2]
            density = 1.0 + 1.5 * sig[block // 2 :]
            modulus = density * speed * speed
            buoyancy = 1.0 / density
            deep_y = 4 * GROUP
            for i in range(4):
                part = slice(i * deep_y, (i + 1) * deep_y)
                mod[4 * a + i, pl.ds(h * deep_y, deep_y)] = modulus[part]
                buoy[VRIM + 4 * a + i, pl.ds(PAD + h * deep_y, deep_y)] = buoyancy[part]
    send(2 * STEPS + 2, every)

    along = [
        split(matrix) for matrix in depth_matrices(size_z)
    ]
    tables = [
        jnp.concatenate(
            [
                jnp.concatenate([high, low], axis=1),
                jnp.concatenate([high, jnp.zeros_like(low)], axis=1),
            ],
            axis=0,
        )
        for high, low in along
    ]

    def along_z(values, table):
        flat = values.reshape(values.shape[0] * size_y, size_z)
        both = mm(jnp.concatenate(split(flat), axis=1), table)
        return (both[:, :size_z] + both[:, size_z:]).reshape(values.shape)

    src_x = place[0:1] - me_x * size_x
    src_y = place[1:2] - me_y * size_y
    at_source = jnp.where(
        (lax.broadcasted_iota(jnp.int32, (size_y, size_z), 0) == src_y)
        & (lax.broadcasted_iota(jnp.int32, (size_y, size_z), 1) == place[2:3]),
        1.0,
        0.0,
    )
    def step(state, way, moment):
        def depth_part(turn, carry):
            here = pl.ds(turn * chunk, chunk)
            inner = press[state, pl.ds(turn * chunk + RIM, chunk), mid_y]
            slope = along_z(inner, tables[0])
            if way == 0:
                slope_z[moment, here] = slope
            moved = vel_z[way, here] - buoy_ref_in(turn) * slope
            vel_z[way, here] = moved
            diverge_z[here] = along_z(moved, tables[1])
            return carry

        def buoy_ref_in(turn):
            return buoy[pl.ds(turn * chunk + VRIM, chunk), mid_y]

        lax.fori_loop(0, size_x // chunk, depth_part, 0)

        if state == 0:
            receive(2 * STEPS + 2)
        if state % STEPS == 0:
            receive(2 * STEPS + way)
        receive(state)

        def along_x(i):
            slope = 0.0
            for order, weight in enumerate(coeffs):
                r = order + 1
                slope = slope + weight * (
                    press[state, i + VRIM - 1 + r, mid_y] - press[state, i + VRIM - r, mid_y]
                )
            vel_x[way, i] = vel_x[way, i] - buoy[i, mid_y] * slope
            return slope

        def ghost_low(i, carry):
            along_x(i)
            return carry

        def faces(x, carry):
            slope = along_x(x + VRIM)
            plane = press[state, x + RIM]
            slope_b = 0.0
            for order, weight in enumerate(coeffs):
                r = order + 1
                back = plane if r == 1 else pltpu.roll(plane, r - 1, 0)
                slope_b = slope_b + weight * (pltpu.roll(plane, tall - r, 0) - back)
            vel_y[way, x] = vel_y[way, x] - buoy[x + VRIM] * slope_b
            if way == 0:
                slope_x[moment, x] = slope
                slope_y[moment, x] = slope_b[PAD : PAD + size_y]
            return carry

        lax.fori_loop(0, VRIM, ghost_low, 0)
        lax.fori_loop(size_x + VRIM, size_x + 2 * VRIM - 1, ghost_low, 0)
        lax.fori_loop(0, size_x, faces, 0, unroll=2)

        def finish(k, carry):
            x = lax.rem(k + size_x - RIM, size_x)
            plane = vel_y[way, x]
            div = diverge_z[x]
            across = 0.0
            for order, weight in enumerate(coeffs):
                r = order + 1
                ahead = plane if r == 1 else pltpu.roll(plane, tall - r + 1, 0)
                across = across + weight * (ahead - pltpu.roll(plane, r, 0))
                div = div + weight * (
                    vel_x[way, x + VRIM + r - 1] - vel_x[way, x + VRIM - r]
                )
            div = div + across[PAD : PAD + size_y]
            value = press[state, x + RIM, mid_y] - mod[x] * div
            if way == 0:
                value = value + at_source * jnp.where(src_x == x, amps[moment : moment + 1], 0.0)
                residue = hits[x] * value - recorded[moment, x]
                div_at[moment, x] = div
                if moment == STEPS - 1:
                    press[state + 1, x + RIM, mid_y] = start_adj[x] + residue
                else:
                    misfit[moment, x] = residue
                    press[state + 1, x + RIM, mid_y] = value
            else:
                part_mod = value * div_at[moment, x]
                part_buoy = (
                    vel_x[way, x + VRIM] * slope_x[moment, x]
                    + plane[PAD : PAD + size_y] * slope_y[moment, x]
                    + vel_z[way, x] * slope_z[moment, x]
                )
                if moment == STEPS - 1:
                    totals[0, x] = -part_mod
                    totals[1, x] = -part_buoy
                else:
                    totals[0, x] = totals[0, x] - part_mod
                    totals[1, x] = totals[1, x] - part_buoy
                if moment > 0:
                    press[state + 1, x + RIM, mid_y] = value + misfit[moment - 1, x]
            return carry

        edge = min(2 * RIM, size_x)
        lax.fori_loop(0, edge, finish, 0, unroll=2)
        more = state + 1 < 2 * STEPS
        if more:
            send(state + 1, (0, 1))
        lax.fori_loop(edge, size_x, finish, 0, unroll=2)
        if more:
            send(state + 1, (2, 3))

    for moment in range(STEPS):
        step(moment, 0, moment)
    for turn in range(STEPS):
        step(STEPS + turn, 1, STEPS - 1 - turn)

    for h in range(halves):
        for a in range(rows_a):
            sig = gates[h, a]
            deep_y = 4 * GROUP
            here = pl.ds(h * deep_y, deep_y)
            grad_mod = jnp.concatenate([totals[0, 4 * a + i, here] for i in range(4)], axis=0)
            grad_buoy = jnp.concatenate([totals[1, 4 * a + i, here] for i in range(4)], axis=0)
            sig_speed, sig_dens = sig[: block // 2], sig[block // 2 :]
            speed = 0.15 + 0.25 * sig_speed
            density = 1.0 + 1.5 * sig_dens
            grad_speed = grad_mod * 2.0 * density * speed
            grad_dens = grad_mod * speed * speed - grad_buoy / (density * density)
            fine = jnp.concatenate(
                [
                    grad_speed * 0.25 * sig_speed * (1.0 - sig_speed),
                    grad_dens * 1.5 * sig_dens * (1.0 - sig_dens),
                ],
                axis=0,
            )
            rows = jnp.transpose(mm2(split(fine), depth_pick, rows_by_rows))
            for k in range(4):
                turned[h, pl.ds(a * cells, cells), k * block : (k + 1) * block] = rows[
                    k * cells : (k + 1) * cells
                ]
    big_gf = 0.0
    big_gs = 0.0
    scatters = []
    for h in range(halves):
        lanes = slice(h * wide, (h + 1) * wide)
        state = hidden[:, lanes]
        outer = split(turned[h])
        grad_pre = mm3(outer, big_second, rows_by_rows) * (1.0 - state * state)
        inner = split(grad_pre)
        grad_rows = mm3(inner, big_first, rows_by_rows)
        for s in range(shots):
            for a in range(rows_a):
                first = a * cells + s * depth_c
                share[s, a, :, lanes] = grad_rows[first : first + depth_c]
        for d in range(1, shots):
            there = axis_peers("shot", d)
            window = pl.ds(h * wide, wide)
            copy = remote(
                share.at[there["shot"], :, :, window],
                landed.at[me, :, :, window],
                shot_send.at[1 + h, d - 1],
                shot_recv.at[1 + h, d - 1],
                there,
            )
            copy.start()
            scatters.append(copy)
        big_gf = big_gf + mm3(split(jnp.transpose(latents[:, lanes])), inner)
        big_gs = big_gs + mm3(split(jnp.transpose(state)), outer)
    landed[me] = share[me]

    sum_f = 0.0
    sum_s = 0.0
    for b in range(GROUP):
        mine = slice(b * CH, (b + 1) * CH)
        sum_f = sum_f + jnp.where(
            one_hot((CH, wide), lambda r, c: c // CH == b), big_gf[mine], 0.0
        )
        sum_s = sum_s + jnp.where(
            one_hot((CH, 4 * block), lambda r, c: c % 16 // 4 == b), big_gs[mine], 0.0
        )
    grad_second = mm2(split(sum_s), order, rows_by_rows)
    grad_first = 0.0
    for side in range(2):
        fold = as_pick(one_hot((wide, outs), lambda r, c: r % CH + side * CH == c))
        grad_first = grad_first + mm2(
            split(sum_f[side * CH // 2 : (side + 1) * CH // 2]), fold
        )
    weights = jnp.concatenate([grad_second, grad_first], axis=0)
    piece = weights.shape[0] // shots
    for s in range(shots):
        w_share[s] = weights[s * piece : (s + 1) * piece]

    def total(stack):
        summed = stack[0]
        for n in range(1, stack.shape[0]):
            summed = summed + stack[n]
        return summed

    hops = [
        remote(
            w_share.at[axis_peers("shot", d)["shot"]],
            w_landed.at[me],
            shot_send.at[1 + halves, d - 1],
            shot_recv.at[1 + halves, d - 1],
            axis_peers("shot", d),
        )
        for d in range(1, shots)
    ]
    for hop in hops:
        hop.start()
    w_landed[me] = w_share[me]
    for hop in hops:
        hop.wait()
    spot = me_x * lax.axis_size("gy") + me_y
    w_plane[spot] = total(w_landed)
    hops = [
        remote(w_plane.at[spot], w_plane.at[spot], plane_send.at[n], plane_recv.at[n], peer)
        for n, peer in enumerate(plane_peers())
    ]
    for hop in hops:
        hop.start()
    for hop in hops:
        hop.wait()
    sums_ref[me] = total(w_plane)
    hops = [
        remote(
            sums_ref.at[me],
            sums_ref.at[me],
            shot_send.at[2 + halves, d - 1],
            shot_recv.at[2 + halves, d - 1],
            axis_peers("shot", d),
        )
        for d in range(1, shots)
    ]
    for hop in hops:
        hop.start()
    for copy in scatters:
        copy.wait()
    own_ref[...] = jnp.transpose(total(landed), (1, 0, 2))
    for hop in hops:
        hop.wait()
    for slot in range(2 * STEPS + 3):
        sent(slot)


def depth_matrices(size_z):
    source = lax.broadcasted_iota(jnp.int32, (size_z, size_z), 0)
    dest = lax.broadcasted_iota(jnp.int32, (size_z, size_z), 1)
    plus = jnp.zeros((size_z, size_z), jnp.float32)
    minus = plus
    for order, weight in enumerate(coeffs):
        r = order + 1
        plus = plus + jnp.where(source == dest + r, weight, 0.0)
        plus = plus - jnp.where(source == dest - r + 1, weight, 0.0)
        minus = minus + jnp.where(source == dest + r - 1, weight, 0.0)
        minus = minus - jnp.where(source == dest - r, weight, 0.0)
    return plus, minus


def finish_kernel(own_ref, sums_ref, latent_ref, first_ref, second_ref, joined):
    latent_ref[...] = own_ref[...]
    piece = sums_ref.shape[1]
    for s in range(sums_ref.shape[0]):
        joined[pl.ds(s * piece, piece)] = sums_ref[s]
    second_ref[...] = joined[pl.ds(0, CH)]
    packed = joined[pl.ds(CH, CH // 2)]
    first_ref[pl.ds(0, CH // 2)] = packed[:, :CH]
    first_ref[pl.ds(CH // 2, CH // 2)] = packed[:, CH:]


def body(
    latent,
    w_first,
    w_second,
    fwd_press,
    fwd_vel,
    adj_press,
    adj_vel,
    src_pos,
    src_amp,
    rec_pos,
    observed,
):
    field = fwd_press.shape[1:]
    size_x, size_y, size_z = field
    tall = size_y + 2 * PAD
    depth_c, rows_a, merged = latent.shape
    cells = size_z // 4
    shots = lax.axis_size("shot")
    tiles = lax.axis_size("gx") * lax.axis_size("gy")
    halves = size_y // (4 * GROUP)
    outs = w_second.shape[1]
    count = rec_pos.shape[2]
    anywhere = pl.BlockSpec(memory_space=pl.ANY)
    vmem = pl.BlockSpec(memory_space=pltpu.VMEM)
    slots = 2 * STEPS + 3
    piece = (CH + CH // 2) // shots

    def scratch(*shape, kind=jnp.float32):
        return pltpu.VMEM(shape, kind)

    def sems(*shape):
        return pltpu.SemaphoreType.DMA(shape)

    own, sums = pl.pallas_call(
        whole_kernel,
        out_shape=(
            jax.ShapeDtypeStruct(latent.shape, jnp.float32),
            jax.ShapeDtypeStruct((shots, piece, outs), jnp.float32),
        ),
        in_specs=[anywhere] * 11,
        out_specs=(vmem, vmem),
        scratch_shapes=[
            scratch(*w_first.shape),
            scratch(*w_second.shape),
            scratch(*src_pos.shape, kind=jnp.int32),
            scratch(*src_amp.shape),
            scratch(3, count, kind=jnp.int32),
            scratch(STEPS, count),
            scratch(*field),
            scratch(shots, *latent.shape),
            scratch(rows_a * cells, merged),
            scratch(rows_a * cells, merged),
            scratch(halves, rows_a, GROUP * outs // 4, size_z),
            scratch(*field),
            scratch(STEPS, *field),
            scratch((2 * STEPS + 1) * size_z, count, kind=half),
            scratch(*field),
            scratch(2 * STEPS, size_x + 2 * RIM, tall, size_z),
            scratch(size_x + 2 * VRIM, tall, size_z),
            scratch(2, size_x + 2 * VRIM, size_y, size_z),
            scratch(2, size_x, tall, size_z),
            scratch(2, *field),
            scratch(*field),
            scratch(STEPS - 1, *field),
            scratch(STEPS, *field),
            scratch(STEPS, *field),
            scratch(STEPS, *field),
            scratch(STEPS, *field),
            scratch(2, *field),
            scratch(halves, rows_a * cells, GROUP * outs),
            scratch(shots, rows_a, depth_c, merged),
            scratch(shots, rows_a, depth_c, merged),
            scratch(shots, piece, outs),
            scratch(shots, piece, outs),
            scratch(tiles, piece, outs),
            sems(15),
            sems(slots, 4),
            sems(slots, 4),
            sems(3 + halves, shots),
            sems(3 + halves, shots),
            sems(tiles),
            sems(tiles),
        ],
        compiler_params=pltpu.CompilerParams(
            collective_id=0, has_side_effects=True, vmem_limit_bytes=60 * 1024 * 1024
        ),
    )(
        latent,
        w_first,
        w_second,
        fwd_press[0],
        fwd_vel[0],
        adj_press[0],
        adj_vel[0],
        src_pos,
        src_amp,
        rec_pos[0],
        observed[0],
    )
    return pl.pallas_call(
        finish_kernel,
        out_shape=(
            jax.ShapeDtypeStruct(latent.shape, jnp.float32),
            jax.ShapeDtypeStruct(w_first.shape, jnp.float32),
            jax.ShapeDtypeStruct(w_second.shape, jnp.float32),
        ),
        scratch_shapes=[scratch(shots * piece, outs)],
    )(own, sums)


def solution(mesh):
    in_specs = (
        P("shot", "gx", "gy"),
        P(),
        P(),
        P("shot", "gx", "gy", None),
        P("shot", None, "gx", "gy", None),
        P("shot", "gx", "gy", None),
        P("shot", None, "gx", "gy", None),
        P(None, "shot"),
        P(None, "shot"),
        P("shot", None, None),
        P("shot", None, None),
    )
    out_specs = (P("shot", "gx", "gy"), P(), P())
    return jax.shard_map(body, mesh=mesh, in_specs=in_specs, out_specs=out_specs, check_vma=False)
```

time: 121 us -> 74.5 us (0.62)
  Pallas kernels: 95.4 us -> 64.9 us
  local copies, waits for them, and re-layouts: 15.2 us -> 8.57 us
  other arithmetic: 4.25 us -> 0 us
  matrix products: 3.55 us -> 0 us
  between operations: 2.11 us -> 0.64 us
    pallas_call x6 -> x2, Pallas kernels: 95.4 us -> 64.9 us  [the longest x1 63.3 us: body(): pl.pallas_call(whole_kernel, out_shape=(jax.ShapeDtypeStruct(latent.shape...]
    unnamed x27 -> x5, local copies, waits for them, and re-layouts: 11 us -> 6.97 us
    dot_general x2 -> x0, matrix products: 3.55 us -> none  [the longest x1 1.82 us: body(): lax.dot_general(everything.reshape(all_depth, rows_x * merged), repeat, (...]
    slice x3 -> x0, local copies, waits for them, and re-layouts: 3.33 us -> none  [the longest x2 2.75 us: body(): return (own.reshape(latent.shape), weights[CH:, :CH], weights[:CH])]
    pallas_call x0 -> x1, local copies, waits for them, and re-layouts: none -> 1.6 us  [body(): pl.pallas_call(finish_kernel, out_shape=(jax.ShapeDtypeStruct(latent.shap...]
    another operation x2 -> x0, other arithmetic: 1.29 us -> none  [the longest x1 1.24 us: body(): jnp.stack([src_pos[0, 0] - anchor_x, src_pos[1, 0] - anchor_y, src_pos[2,...]
where the time goes in v1:
time: 74.5 us; the launch traced here: 74.1 us
  Pallas kernels  64.9 us (87%)
  local copies, waits for them, and re-layouts  8.57 us (12%)
    pallas_call x1, Pallas kernels, body(): pl.pallas_call(whole_kernel, out_shape=(jax.ShapeDtypeStruct(latent.shape...  63.3 us
    unnamed x5, local copies, waits for them, and re-layouts  6.97 us
    pallas_call x1, Pallas kernels, body(): pl.pallas_call(finish_kernel, out_shape=(jax.ShapeDtypeStruct(latent.shap...  1.6 us
    pallas_call x1, local copies, waits for them, and re-layouts, body(): pl.pallas_call(finish_kernel, out_shape=(jax.ShapeDtypeStruct(latent.shap...  1.6 us

profile of v1, /device:TPU:0, one launch (start us, length us, event | category | flops | bytes accessed | tf_op | source)
XLA Modules:
  0.0 74.1 jit_solution(9686464418924653756)
XLA Ops:
  0.6 1.3 %copy.15.src_pos = s32[3,1]{1,0:T(4,128)} copy(s32[3,1]{0,1:T(1,128)} %param.18) | data formatting | bytes 24 | tf_op args[7]
  1.9 1.3 %copy.16.src_amp = f32[3,1]{1,0:T(4,128)} copy(f32[3,1]{0,1:T(1,128)} %param.19) | data formatting | bytes 24 | tf_op args[8]
  3.3 1.4 %copy.23 = s32[1,3,2048]{2,1,0:T(4,128)} copy(s32[1,3,2048]{2,0,1:T(1,128)} %param.20) | data formatting | bytes 49152
  4.6 1.4 %copy.22 = f32[1,3,2048]{2,1,0:T(4,128)} copy(f32[1,3,2048]{2,0,1:T(1,128)} %param.21) | data formatting | bytes 49152
  6.0 1.6 %copy.14.latent_ref = f32[8,6,512]{2,1,0:T(8,128)} copy(f32[8,6,512]{2,0,1:T(8,128)} %param.11) | data formatting | bytes 196608 | tf_op args[0]
  7.6 63.3 %shard_map.130 = (f32[8,6,512]{2,1,0:T(8,128)}, f32[4,24,128]{2,1,0:T(8,128)}) custom-call(f32[8,6,512]{2,1,0:T(8,128)} %copy.14.latent_ref, f32[64,64]{1,0:T(8,128)} %first_ref.1, f32[64,128]{1,0:T(8,128)} %second_ref.1, f32[24,32,128]{2,1,0:T(8,128)} %bitcast.12, f32[3,24,32,128]{3,2,1,0:T(8,128)} %bitcast.10, f32[24,32,128]{2,1,0:T(8,128)} %bitcast.13, ...), custom_call_target="tpu_custom_call" | custom-call | tf_op jit(solution)/shard_map/pallas_call | solution.py:731
  70.9 1.6 %shard_map.131 = (f32[8,6,512]{2,1,0:T(8,128)}, f32[64,64]{1,0:T(8,128)}, f32[64,128]{1,0:T(8,128)}) custom-call(f32[8,6,512]{2,1,0:T(8,128)} %get-tuple-element.5.own_ref, f32[4,24,128]{2,1,0:T(8,128)} %get-tuple-element.6.sums_ref), custom_call_target="tpu_custom_call" | custom-call | tf_op jit(solution)/shard_map/pallas_call | solution.py:797
  72.5 1.6 %copy.17 = f32[8,6,512]{2,0,1:T(8,128)} copy(f32[8,6,512]{2,1,0:T(8,128)} %get-tuple-element.7) | data formatting | bytes 196608 | tf_op jit(solution)/shard_map/pallas_call | solution.py:797

commit v2 on v1

--- a/solution.py
+++ b/solution.py
@@ -116,7 +116,9 @@
     rec_weights,
     mod,
     press,
-    buoy,
+    buoy_x,
+    buoy_y,
+    kicks,
     vel_x,
     vel_y,
     vel_z,
@@ -143,7 +145,6 @@
 ):
     size_x, size_y, size_z = mod.shape
     cells = size_z // 4
-    tall = size_y + 2 * PAD
     mid_y = pl.ds(PAD, size_y)
     mid_v = pl.ds(VRIM, size_x)
     rows_a = size_x // 4
@@ -181,7 +182,7 @@
     ]
     for way, vel in enumerate((fwd_vel, adj_vel)):
         loads.append((vel.at[0], vel_x.at[way, pl.ds(VRIM, size_x)]))
-        loads.append((vel.at[1], vel_y.at[way, :, mid_y]))
+        loads.append((vel.at[1], vel_y.at[way, :, pl.ds(VRIM, size_y)]))
         loads.append((vel.at[2], vel_z.at[way]))
     moves = [
         pltpu.make_async_copy(source, dest, local_sem.at[n])
@@ -190,91 +191,103 @@
     for move in moves:
         move.start()
 
-    def channel(slot, pairs):
-        return [
-            remote(
-                pairs[side][0],
-                pairs[side][1],
-                send_sem.at[slot, side],
-                recv_sem.at[slot, side ^ 1],
-                target[side],
+    class Link:
+        def __init__(self, slot, pairs):
+            self.copies = {
+                side: remote(
+                    *pair,
+                    send_sem.at[slot, side],
+                    recv_sem.at[slot, side ^ 1],
+                    target[side],
+                )
+                for side, pair in pairs.items()
+            }
+
+        def send(self, *sides):
+            for side in sides or self.copies:
+                pl.when(has[side])(self.copies[side].start)
+
+        def receive(self, *sides):
+            for side in sides or self.copies:
+                pl.when(has[side])(self.copies[side ^ 1].wait_recv)
+
+        def sent(self):
+            for side in self.copies:
+                pl.when(has[side])(self.copies[side].wait_send)
+
+    def x_pairs(low, high, dest, rim):
+        return {0: (low, dest(size_x + rim, rim)), 1: (high, dest(0, rim))}
+
+    def y_pairs(low, high, dest, at_low, at_high):
+        return {2: (low, dest(at_high)), 3: (high, dest(at_low))}
+
+    slot = 0
+    links_x, links_y = [], []
+    spans = (pl.ds(0, RIM), pl.ds(size_x - RIM, RIM), pl.ds(RIM, size_x - 2 * RIM))
+    inner = (pl.ds(RIM, RIM), pl.ds(size_x, RIM), pl.ds(2 * RIM, size_x - 2 * RIM))
+    for state in range(2 * STEPS):
+
+        def plane(first, count, state=state):
+            return press.at[state, pl.ds(first, count), mid_y]
+
+        low, high = plane(RIM, RIM), plane(size_x, RIM)
+        if state == 0:
+            low, high = fwd_press.at[spans[0]], fwd_press.at[spans[1]]
+        links_x.append(Link(slot, x_pairs(low, high, plane, RIM)))
+        slot += 1
+        parts = []
+        for span, rows in zip(spans, inner):
+
+            def strip(first, state=state, rows=rows):
+                return press.at[state, rows, pl.ds(first, PAD)]
+
+            low, high = strip(PAD), strip(size_y)
+            if state == 0:
+                low = fwd_press.at[span, pl.ds(0, PAD)]
+                high = fwd_press.at[span, pl.ds(size_y - PAD, PAD)]
+            parts.append(Link(slot, y_pairs(low, high, strip, 0, size_y + PAD)))
+            slot += 1
+        links_y.append(parts)
+
+    def strips(ref):
+        return lambda first: ref.at[:, pl.ds(first, VRIM)]
+
+    def layers(ref):
+        return lambda first, count: ref.at[pl.ds(first, count)]
+
+    vel_links = []
+    for way, vel in enumerate((fwd_vel, adj_vel)):
+        pairs = x_pairs(
+            vel.at[0, pl.ds(0, VRIM)],
+            vel.at[0, pl.ds(size_x - VRIM, VRIM)],
+            layers(vel_x.at[way]),
+            VRIM,
+        )
+        pairs.update(
+            y_pairs(
+                vel.at[1, :, pl.ds(0, VRIM)],
+                vel.at[1, :, pl.ds(size_y - VRIM, VRIM)],
+                strips(vel_y.at[way]),
+                0,
+                size_y + VRIM,
             )
-            for side in range(4)
-        ]
-
-    def press_pairs(state, edges):
-        low_x, high_x = pl.ds(0, RIM), pl.ds(size_x + RIM, RIM)
-        low_y, high_y = pl.ds(0, PAD), pl.ds(size_y + PAD, PAD)
-        mid_x = pl.ds(RIM, size_x)
-        return [
-            (edges[0], press.at[state, high_x, mid_y]),
-            (edges[1], press.at[state, low_x, mid_y]),
-            (edges[2], press.at[state, mid_x, high_y]),
-            (edges[3], press.at[state, mid_x, low_y]),
-        ]
-
-    def own_edges(state):
-        mid_x = pl.ds(RIM, size_x)
-        return [
-            press.at[state, pl.ds(RIM, RIM), mid_y],
-            press.at[state, pl.ds(size_x, RIM), mid_y],
-            press.at[state, mid_x, pl.ds(PAD, PAD)],
-            press.at[state, mid_x, pl.ds(size_y, PAD)],
-        ]
-
-    first_edges = [
-        fwd_press.at[pl.ds(0, RIM)],
-        fwd_press.at[pl.ds(size_x - RIM, RIM)],
-        fwd_press.at[:, pl.ds(0, PAD)],
-        fwd_press.at[:, pl.ds(size_y - PAD, PAD)],
-    ]
-    channels = [channel(0, press_pairs(0, first_edges))]
-    for state in range(1, 2 * STEPS):
-        channels.append(channel(state, press_pairs(state, own_edges(state))))
-    for way, vel in enumerate((fwd_vel, adj_vel)):
-        channels.append(
-            channel(
-                2 * STEPS + way,
-                [
-                    (vel.at[0, pl.ds(0, VRIM)], vel_x.at[way, pl.ds(size_x + VRIM, VRIM)]),
-                    (vel.at[0, pl.ds(size_x - VRIM, VRIM)], vel_x.at[way, pl.ds(0, VRIM)]),
-                    (vel.at[1, :, pl.ds(0, PAD)], vel_y.at[way, :, pl.ds(size_y + PAD, PAD)]),
-                    (vel.at[1, :, pl.ds(size_y - PAD, PAD)], vel_y.at[way, :, pl.ds(0, PAD)]),
-                ],
-            )
-        )
-    channels.append(
-        channel(
-            2 * STEPS + 2,
-            [
-                (buoy.at[pl.ds(VRIM, VRIM), mid_y], buoy.at[pl.ds(size_x + VRIM, VRIM), mid_y]),
-                (buoy.at[pl.ds(size_x, VRIM), mid_y], buoy.at[pl.ds(0, VRIM), mid_y]),
-                (buoy.at[mid_v, pl.ds(PAD, PAD)], buoy.at[mid_v, pl.ds(size_y + PAD, PAD)]),
-                (buoy.at[mid_v, pl.ds(size_y, PAD)], buoy.at[mid_v, pl.ds(0, PAD)]),
-            ],
-        )
-    )
-
-    def send(slot, sides):
-        for side in sides:
-
-            @pl.when(has[side])
-            def _():
-                channels[slot][side].start()
-
-    def receive(slot):
-        for side in range(4):
-
-            @pl.when(has[side])
-            def _():
-                channels[slot][side ^ 1].wait_recv()
-
-    def sent(slot):
-        for side in range(4):
-
-            @pl.when(has[side])
-            def _():
-                channels[slot][side].wait_send()
+        )
+        vel_links.append(Link(slot, pairs))
+        slot += 1
+    pairs = x_pairs(
+        buoy_x.at[pl.ds(VRIM, VRIM)], buoy_x.at[pl.ds(size_x, VRIM)], layers(buoy_x), VRIM
+    )
+    pairs.update(
+        y_pairs(
+            buoy_y.at[:, pl.ds(VRIM, VRIM)],
+            buoy_y.at[:, pl.ds(size_y, VRIM)],
+            strips(buoy_y),
+            0,
+            size_y + VRIM,
+        )
+    )
+    buoy_link = Link(slot, pairs)
+    links = [*links_x, *sum(links_y, []), *vel_links, buoy_link]
 
     for side in range(4):
 
@@ -286,17 +299,21 @@
                 vrows = pl.ds(far * (size_x + VRIM), VRIM)
                 for state in range(2 * STEPS):
                     press[state, rows, mid_y] = jnp.zeros((RIM, size_y, size_z), jnp.float32)
-                buoy[vrows, mid_y] = jnp.zeros((VRIM, size_y, size_z), jnp.float32)
+                blank = jnp.zeros((VRIM, size_y, size_z), jnp.float32)
+                buoy_x[vrows] = blank
                 for way in range(2):
-                    vel_x[way, vrows] = jnp.zeros((VRIM, size_y, size_z), jnp.float32)
+                    vel_x[way, vrows] = blank
             else:
                 cols = pl.ds(far * (size_y + PAD), PAD)
-                blank = jnp.zeros((size_x, PAD, size_z), jnp.float32)
                 for state in range(2 * STEPS):
-                    press[state, pl.ds(RIM, size_x), cols] = blank
-                buoy[mid_v, cols] = blank
+                    press[state, pl.ds(RIM, size_x), cols] = jnp.zeros(
+                        (size_x, PAD, size_z), jnp.float32
+                    )
+                vcols = pl.ds(far * (size_y + VRIM), VRIM)
+                blank = jnp.zeros((size_x, VRIM, size_z), jnp.float32)
+                buoy_y[:, vcols] = blank
                 for way in range(2):
-                    vel_y[way, :, cols] = blank
+                    vel_y[way, :, vcols] = blank
 
     pl.semaphore_wait(barrier, greeted)
 
@@ -312,10 +329,8 @@
     ]
     for copy in gathers:
         copy.start()
-    every = range(4)
-    send(0, every)
-    send(2 * STEPS, every)
-    send(2 * STEPS + 1, every)
+    for link in (links_x[0], *links_y[0], *vel_links):
+        link.send()
     for move in moves:
         move.wait()
 
@@ -340,17 +355,17 @@
     )
     depth_pick = as_pick(one_hot((size_z, size_z), lambda r, c: 4 * (r % cells) + r // cells == c))
 
-    count = rec_at.shape[1]
-    local_x = rec_at[0:1] - me_x * size_x
-    local_y = rec_at[1:2] - me_y * size_y
+    count = rec_at.shape[2]
+    local_x = rec_at[0] - me_x * size_x
+    local_y = rec_at[1] - me_y * size_y
     inside = (local_x >= 0) & (local_x < size_x) & (local_y >= 0) & (local_y < size_y)
     column = jnp.where(inside, local_x * size_y + local_y, -1)
     deep = jnp.where(
-        lax.broadcasted_iota(jnp.int32, (size_z, count), 0) == rec_at[2:3], 1.0, 0.0
+        lax.broadcasted_iota(jnp.int32, (size_z, count), 0) == rec_at[2], 1.0, 0.0
     )
     rec_weights[pl.ds(0, size_z)] = deep.astype(half)
     for moment in range(STEPS):
-        for part, values in enumerate(split(seen[moment : moment + 1])):
+        for part, values in enumerate(split(seen[moment])):
             rec_weights[pl.ds((1 + 2 * moment + part) * size_z, size_z)] = (
                 deep * values.astype(jnp.float32)
             ).astype(half)
@@ -374,13 +389,26 @@
 
     lax.fori_loop(0, size_x // chunk, planes, 0)
 
+    src_x = place[:, 0:1] - me_x * size_x
+    src_y = place[:, 1:2] - me_y * size_y
+    at_source = (lax.broadcasted_iota(jnp.int32, (size_y, size_z), 0) == src_y) & (
+        lax.broadcasted_iota(jnp.int32, (size_y, size_z), 1) == place[:, 2:3]
+    )
+    impulses = [jnp.where(at_source, amps[:, n : n + 1], 0.0) for n in range(STEPS)]
+
+    def kick(x, carry):
+        for n in range(STEPS):
+            kicks[n, x] = jnp.where(src_x == x, impulses[n], 0.0)
+        return carry
+
+    lax.fori_loop(0, size_x, kick, 0)
+
     for copy in gathers:
         copy.wait()
-    depth_c = slabs.shape[1]
+    depth_c = slabs.shape[2]
     for s in range(shots):
-        slab = jnp.transpose(slabs[s], (1, 0, 2))
         for a in range(rows_a):
-            latents[pl.ds(a * cells + s * depth_c, depth_c)] = slab[a]
+            latents[pl.ds(a * cells + s * depth_c, depth_c)] = slabs[s, a]
     for h in range(halves):
         lanes = slice(h * wide, (h + 1) * wide)
         state = jnp.tanh(mm3(split(latents[:, lanes]), big_first))
@@ -401,8 +429,9 @@
             for i in range(4):
                 part = slice(i * deep_y, (i + 1) * deep_y)
                 mod[4 * a + i, pl.ds(h * deep_y, deep_y)] = modulus[part]
-                buoy[VRIM + 4 * a + i, pl.ds(PAD + h * deep_y, deep_y)] = buoyancy[part]
-    send(2 * STEPS + 2, every)
+                buoy_x[VRIM + 4 * a + i, pl.ds(h * deep_y, deep_y)] = buoyancy[part]
+                buoy_y[4 * a + i, pl.ds(VRIM + h * deep_y, deep_y)] = buoyancy[part]
+    buoy_link.send()
 
     along = [
         split(matrix) for matrix in depth_matrices(size_z)
@@ -418,122 +447,135 @@
         for high, low in along
     ]
 
+    low_rows, high_rows = (0, RIM), (size_x - RIM, size_x)
+    mid_rows = (RIM, size_x - RIM)
+    columns = size_y // 8
+
+    def column_of(c, base):
+        return pl.ds(pl.multiple_of(8 * c, 8) + base, 8)
+
+    def weigh(ahead, behind):
+        summed = 0.0
+        for order_at, weight in enumerate(coeffs):
+            summed = summed + weight * (ahead[order_at] - behind[order_at])
+        return summed
+
     def along_z(values, table):
-        flat = values.reshape(values.shape[0] * size_y, size_z)
+        flat = values.reshape(size_x * size_y, size_z)
         both = mm(jnp.concatenate(split(flat), axis=1), table)
         return (both[:, :size_z] + both[:, size_z:]).reshape(values.shape)
 
-    src_x = place[0:1] - me_x * size_x
-    src_y = place[1:2] - me_y * size_y
-    at_source = jnp.where(
-        (lax.broadcasted_iota(jnp.int32, (size_y, size_z), 0) == src_y)
-        & (lax.broadcasted_iota(jnp.int32, (size_y, size_z), 1) == place[2:3]),
-        1.0,
-        0.0,
-    )
+    def depth_part(state, way, moment):
+        slope = along_z(press[state, pl.ds(RIM, size_x), mid_y], tables[0])
+        if way == 0:
+            slope_z[moment] = slope
+        moved = vel_z[way] - buoy_x[mid_v] * slope
+        vel_z[way] = moved
+        diverge_z[...] = along_z(moved, tables[1])
+
+    def faces_x(state, way, moment, first, last):
+        def one(c, carry):
+            here, there = column_of(c, 0), column_of(c, PAD)
+            rows = {
+                i: press[state, i + RIM, there] for i in range(first - 3, last + 4)
+            }
+            for x in range(first, last):
+                slope = weigh([rows[x + r] for r in (1, 2, 3, 4)], [rows[x - r + 1] for r in (1, 2, 3, 4)])
+                vel_x[way, x + VRIM, here] = (
+                    vel_x[way, x + VRIM, here] - buoy_x[x + VRIM, here] * slope
+                )
+                if way == 0 and 0 <= x < size_x:
+                    slope_x[moment, x, here] = slope
+            return carry
+
+        lax.fori_loop(0, columns, one, 0)
+
+    def faces_y(state, way, moment, rows):
+        def one(x, carry):
+            def at(r):
+                return press[state, x + RIM, pl.ds(VRIM + r, size_y + 2 * VRIM)]
+
+            slope = weigh([at(r) for r in (1, 2, 3, 4)], [at(1 - r) for r in (1, 2, 3, 4)])
+            vel_y[way, x] = vel_y[way, x] - buoy_y[x] * slope
+            if way == 0:
+                slope_y[moment, x] = slope
+            return carry
+
+        lax.fori_loop(rows[0], rows[1], one, 0, unroll=2)
+
+    def finish(state, way, moment, rows):
+        first, last = rows
+
+        def one(c, carry):
+            here, there = column_of(c, 0), column_of(c, PAD)
+            speeds = {
+                i: vel_x[way, i + VRIM, here] for i in range(first - VRIM, last + VRIM - 1)
+            }
+
+            def at(x, r):
+                return vel_y[way, x, column_of(c, VRIM + r)]
+
+            for x in range(first, last):
+                div = diverge_z[x, here] + weigh(
+                    [speeds[x + r - 1] for r in (1, 2, 3, 4)], [speeds[x - r] for r in (1, 2, 3, 4)]
+                )
+                div = div + weigh(
+                    [at(x, r - 1) for r in (1, 2, 3, 4)], [at(x, -r) for r in (1, 2, 3, 4)]
+                )
+                value = press[state, x + RIM, there] - mod[x, here] * div
+                if way == 0:
+                    value = value + kicks[moment, x, here]
+                    residue = hits[x, here] * value - recorded[moment, x, here]
+                    div_at[moment, x, here] = div
+                    if moment == STEPS - 1:
+                        press[state + 1, x + RIM, there] = start_adj[x, here] + residue
+                    else:
+                        misfit[moment, x, here] = residue
+                        press[state + 1, x + RIM, there] = value
+                else:
+                    part_mod = value * div_at[moment, x, here]
+                    part_buoy = (
+                        speeds[x] * slope_x[moment, x, here]
+                        + at(x, 0) * slope_y[moment, x, column_of(c, VRIM)]
+                        + vel_z[way, x, here] * slope_z[moment, x, here]
+                    )
+                    if moment == STEPS - 1:
+                        totals[0, x, here] = -part_mod
+                        totals[1, x, here] = -part_buoy
+                    else:
+                        totals[0, x, here] = totals[0, x, here] - part_mod
+                        totals[1, x, here] = totals[1, x, here] - part_buoy
+                    if moment > 0:
+                        press[state + 1, x + RIM, there] = value + misfit[moment - 1, x, here]
+            return carry
+
+        lax.fori_loop(0, columns, one, 0)
+
     def step(state, way, moment):
-        def depth_part(turn, carry):
-            here = pl.ds(turn * chunk, chunk)
-            inner = press[state, pl.ds(turn * chunk + RIM, chunk), mid_y]
-            slope = along_z(inner, tables[0])
-            if way == 0:
-                slope_z[moment, here] = slope
-            moved = vel_z[way, here] - buoy_ref_in(turn) * slope
-            vel_z[way, here] = moved
-            diverge_z[here] = along_z(moved, tables[1])
-            return carry
-
-        def buoy_ref_in(turn):
-            return buoy[pl.ds(turn * chunk + VRIM, chunk), mid_y]
-
-        lax.fori_loop(0, size_x // chunk, depth_part, 0)
-
+        depth_part(state, way, moment)
+        faces_x(state, way, moment, 3, size_x - 4)
         if state == 0:
-            receive(2 * STEPS + 2)
+            buoy_link.receive()
         if state % STEPS == 0:
-            receive(2 * STEPS + way)
-        receive(state)
-
-        def along_x(i):
-            slope = 0.0
-            for order, weight in enumerate(coeffs):
-                r = order + 1
-                slope = slope + weight * (
-                    press[state, i + VRIM - 1 + r, mid_y] - press[state, i + VRIM - r, mid_y]
-                )
-            vel_x[way, i] = vel_x[way, i] - buoy[i, mid_y] * slope
-            return slope
-
-        def ghost_low(i, carry):
-            along_x(i)
-            return carry
-
-        def faces(x, carry):
-            slope = along_x(x + VRIM)
-            plane = press[state, x + RIM]
-            slope_b = 0.0
-            for order, weight in enumerate(coeffs):
-                r = order + 1
-                back = plane if r == 1 else pltpu.roll(plane, r - 1, 0)
-                slope_b = slope_b + weight * (pltpu.roll(plane, tall - r, 0) - back)
-            vel_y[way, x] = vel_y[way, x] - buoy[x + VRIM] * slope_b
-            if way == 0:
-                slope_x[moment, x] = slope
-                slope_y[moment, x] = slope_b[PAD : PAD + size_y]
-            return carry
-
-        lax.fori_loop(0, VRIM, ghost_low, 0)
-        lax.fori_loop(size_x + VRIM, size_x + 2 * VRIM - 1, ghost_low, 0)
-        lax.fori_loop(0, size_x, faces, 0, unroll=2)
-
-        def finish(k, carry):
-            x = lax.rem(k + size_x - RIM, size_x)
-            plane = vel_y[way, x]
-            div = diverge_z[x]
-            across = 0.0
-            for order, weight in enumerate(coeffs):
-                r = order + 1
-                ahead = plane if r == 1 else pltpu.roll(plane, tall - r + 1, 0)
-                across = across + weight * (ahead - pltpu.roll(plane, r, 0))
-                div = div + weight * (
-                    vel_x[way, x + VRIM + r - 1] - vel_x[way, x + VRIM - r]
-                )
-            div = div + across[PAD : PAD + size_y]
-            value = press[state, x + RIM, mid_y] - mod[x] * div
-            if way == 0:
-                value = value + at_source * jnp.where(src_x == x, amps[moment : moment + 1], 0.0)
-                residue = hits[x] * value - recorded[moment, x]
-                div_at[moment, x] = div
-                if moment == STEPS - 1:
-                    press[state + 1, x + RIM, mid_y] = start_adj[x] + residue
-                else:
-                    misfit[moment, x] = residue
-                    press[state + 1, x + RIM, mid_y] = value
-            else:
-                part_mod = value * div_at[moment, x]
-                part_buoy = (
-                    vel_x[way, x + VRIM] * slope_x[moment, x]
-                    + plane[PAD : PAD + size_y] * slope_y[moment, x]
-                    + vel_z[way, x] * slope_z[moment, x]
-                )
-                if moment == STEPS - 1:
-                    totals[0, x] = -part_mod
-                    totals[1, x] = -part_buoy
-                else:
-                    totals[0, x] = totals[0, x] - part_mod
-                    totals[1, x] = totals[1, x] - part_buoy
-                if moment > 0:
-                    press[state + 1, x + RIM, mid_y] = value + misfit[moment - 1, x]
-            return carry
-
-        edge = min(2 * RIM, size_x)
-        lax.fori_loop(0, edge, finish, 0, unroll=2)
+            vel_links[way].receive()
+        ends = [(0, low_rows, (-VRIM, 3)), (1, high_rows, (size_x - 4, size_x + 3))]
+        if state % 2:
+            ends.reverse()
         more = state + 1 < 2 * STEPS
+        for side, rows, ghosts in ends:
+            links_x[state].receive(side)
+            links_y[state][side].receive()
+            faces_x(state, way, moment, *ghosts)
+            faces_y(state, way, moment, rows)
+            finish(state, way, moment, rows)
+            if more:
+                links_x[state + 1].send(side)
+                links_y[state + 1][side].send()
+        links_y[state][2].receive()
+        faces_y(state, way, moment, mid_rows)
+        finish(state, way, moment, mid_rows)
         if more:
-            send(state + 1, (0, 1))
-        lax.fori_loop(edge, size_x, finish, 0, unroll=2)
-        if more:
-            send(state + 1, (2, 3))
+            links_y[state + 1][2].send()
 
     for moment in range(STEPS):
         step(moment, 0, moment)
@@ -662,11 +704,11 @@
         hop.start()
     for copy in scatters:
         copy.wait()
-    own_ref[...] = jnp.transpose(total(landed), (1, 0, 2))
+    own_ref[...] = total(landed)
     for hop in hops:
         hop.wait()
-    for slot in range(2 * STEPS + 3):
-        sent(slot)
+    for link in links:
+        link.sent()
 
 
 def depth_matrices(size_z):
@@ -719,7 +761,7 @@
     count = rec_pos.shape[2]
     anywhere = pl.BlockSpec(memory_space=pl.ANY)
     vmem = pl.BlockSpec(memory_space=pltpu.VMEM)
-    slots = 2 * STEPS + 3
+    slots = 4 * 2 * STEPS + 3
     piece = (CH + CH // 2) // shots
 
     def scratch(*shape, kind=jnp.float32):
@@ -731,7 +773,7 @@
     own, sums = pl.pallas_call(
         whole_kernel,
         out_shape=(
-            jax.ShapeDtypeStruct(latent.shape, jnp.float32),
+            jax.ShapeDtypeStruct((rows_a, depth_c, merged), jnp.float32),
             jax.ShapeDtypeStruct((shots, piece, outs), jnp.float32),
         ),
         in_specs=[anywhere] * 11,
@@ -739,12 +781,12 @@
         scratch_shapes=[
             scratch(*w_first.shape),
             scratch(*w_second.shape),
-            scratch(*src_pos.shape, kind=jnp.int32),
-            scratch(*src_amp.shape),
-            scratch(3, count, kind=jnp.int32),
-            scratch(STEPS, count),
+            scratch(*src_pos.shape[::-1], kind=jnp.int32),
+            scratch(*src_amp.shape[::-1]),
+            scratch(3, 1, count, kind=jnp.int32),
+            scratch(STEPS, 1, count),
             scratch(*field),
-            scratch(shots, *latent.shape),
+            scratch(shots, rows_a, depth_c, merged),
             scratch(rows_a * cells, merged),
             scratch(rows_a * cells, merged),
             scratch(halves, rows_a, GROUP * outs // 4, size_z),
@@ -753,15 +795,17 @@
             scratch((2 * STEPS + 1) * size_z, count, kind=half),
             scratch(*field),
             scratch(2 * STEPS, size_x + 2 * RIM, tall, size_z),
-            scratch(size_x + 2 * VRIM, tall, size_z),
+            scratch(size_x + 2 * VRIM, size_y, size_z),
+            scratch(size_x, size_y + 2 * VRIM, size_z),
+            scratch(STEPS, *field),
             scratch(2, size_x + 2 * VRIM, size_y, size_z),
-            scratch(2, size_x, tall, size_z),
+            scratch(2, size_x, size_y + 2 * VRIM, size_z),
             scratch(2, *field),
             scratch(*field),
             scratch(STEPS - 1, *field),
             scratch(STEPS, *field),
             scratch(STEPS, *field),
-            scratch(STEPS, *field),
+            scratch(STEPS, size_x, size_y + 2 * VRIM, size_z),
             scratch(STEPS, *field),
             scratch(2, *field),
             scratch(halves, rows_a * cells, GROUP * outs),
@@ -782,27 +826,28 @@
             collective_id=0, has_side_effects=True, vmem_limit_bytes=60 * 1024 * 1024
         ),
     )(
-        latent,
+        latent.transpose(1, 0, 2),
         w_first,
         w_second,
         fwd_press[0],
         fwd_vel[0],
         adj_press[0],
         adj_vel[0],
-        src_pos,
-        src_amp,
-        rec_pos[0],
-        observed[0],
-    )
-    return pl.pallas_call(
+        src_pos.T,
+        src_amp.T,
+        rec_pos.transpose(1, 0, 2),
+        observed.transpose(1, 0, 2),
+    )
+    grad_latent, grad_first, grad_second = pl.pallas_call(
         finish_kernel,
         out_shape=(
-            jax.ShapeDtypeStruct(latent.shape, jnp.float32),
+            jax.ShapeDtypeStruct(own.shape, jnp.float32),
             jax.ShapeDtypeStruct(w_first.shape, jnp.float32),
             jax.ShapeDtypeStruct(w_second.shape, jnp.float32),
         ),
         scratch_shapes=[scratch(shots * piece, outs)],
     )(own, sums)
+    return grad_latent.transpose(1, 0, 2), grad_first, grad_second
 
 
 def solution(mesh):

time: 74.5 us -> 61.1 us (0.82)
  local copies, waits for them, and re-layouts: 8.57 us -> 0 us
  Pallas kernels: 64.9 us -> 60.3 us
    unnamed x5 -> x0, local copies, waits for them, and re-layouts: 6.97 us -> none
    pallas_call x2, Pallas kernels: 64.9 us -> 60.3 us  [the longest x1 58.7 us: body(): pl.pallas_call(whole_kernel, out_shape=(jax.ShapeDtypeStruct((rows_a, dep...]
    pallas_call x1 -> x0, local copies, waits for them, and re-layouts: 1.6 us -> none  [body(): pl.pallas_call(finish_kernel, out_shape=(jax.ShapeDtypeStruct(latent.shap...]
where the time goes in v2:
time: 61.1 us; the launch traced here: 61 us
  Pallas kernels  60.3 us (99%)
  between operations  0.64 us (1%)
    pallas_call x1, Pallas kernels, body(): pl.pallas_call(whole_kernel, out_shape=(jax.ShapeDtypeStruct((rows_a, dep...  58.7 us
    pallas_call x1, Pallas kernels, body(): pl.pallas_call(finish_kernel, out_shape=(jax.ShapeDtypeStruct(own.shape,...  1.59 us

profile of v2, /device:TPU:0, one launch (start us, length us, event | category | flops | bytes accessed | tf_op | source)
XLA Modules:
  0.0 61.0 jit_solution(14509002653948953909)
XLA Ops:
  0.6 58.7 %shard_map.130 = (f32[6,8,512]{2,1,0:T(8,128)}, f32[4,24,128]{2,1,0:T(8,128)}) custom-call(f32[6,8,512]{2,1,0:T(8,128)} %bitcast.14, f32[64,64]{1,0:T(8,128)} %first_ref.1, f32[64,128]{1,0:T(8,128)} %second_ref.1, f32[24,32,128]{2,1,0:T(8,128)} %bitcast.12, f32[3,24,32,128]{3,2,1,0:T(8,128)} %bitcast.10, f32[24,32,128]{2,1,0:T(8,128)} %bitcast.13, ...), custom_call_target="tpu_custom_call" | custom-call | tf_op jit(solution)/shard_map/pallas_call | solution.py:773
  59.4 1.6 %shard_map.131 = (f32[6,8,512]{2,1,0:T(8,128)}, f32[64,64]{1,0:T(8,128)}, f32[64,128]{1,0:T(8,128)}) custom-call(f32[6,8,512]{2,1,0:T(8,128)} %get-tuple-element.8.own_ref, f32[4,24,128]{2,1,0:T(8,128)} %get-tuple-element.9.sums_ref), custom_call_target="tpu_custom_call" | custom-call | tf_op jit(solution)/shard_map/pallas_call | solution.py:841

commit v3 on v2

--- a/solution.py
+++ b/solution.py
@@ -11,6 +11,7 @@
 VRIM = 4
 PAD = 8
 GROUP = 4
+PARTS = 2
 LANES = 128
 
 coeffs = (1225.0 / 1024.0, -245.0 / 3072.0, 49.0 / 5120.0, -5.0 / 7168.0)
@@ -131,6 +132,8 @@
     totals,
     turned,
     share,
+    paired,
+    summed,
     landed,
     w_share,
     w_landed,
@@ -170,13 +173,13 @@
         greeted += 1
 
     loads = [
+        (latent_ref, slabs.at[me]),
         (first_ref, w_first),
         (second_ref, w_second),
         (rec_pos, rec_at),
         (observed, seen),
         (src_pos, place),
         (src_amp, amps),
-        (latent_ref, slabs.at[me]),
         (fwd_press, press.at[0, pl.ds(RIM, size_x), mid_y]),
         (adj_press, start_adj),
     ]
@@ -223,18 +226,25 @@
 
     slot = 0
     links_x, links_y = [], []
+    deep_part = size_y // PARTS
     spans = (pl.ds(0, RIM), pl.ds(size_x - RIM, RIM), pl.ds(RIM, size_x - 2 * RIM))
     inner = (pl.ds(RIM, RIM), pl.ds(size_x, RIM), pl.ds(2 * RIM, size_x - 2 * RIM))
     for state in range(2 * STEPS):
-
-        def plane(first, count, state=state):
-            return press.at[state, pl.ds(first, count), mid_y]
-
-        low, high = plane(RIM, RIM), plane(size_x, RIM)
-        if state == 0:
-            low, high = fwd_press.at[spans[0]], fwd_press.at[spans[1]]
-        links_x.append(Link(slot, x_pairs(low, high, plane, RIM)))
-        slot += 1
+        parts = []
+        for part in range(PARTS):
+            inside = pl.ds(part * deep_part, deep_part)
+
+            def plane(first, count, state=state, part=part):
+                return press.at[
+                    state, pl.ds(first, count), pl.ds(PAD + part * deep_part, deep_part)
+                ]
+
+            low, high = plane(RIM, RIM), plane(size_x, RIM)
+            if state == 0:
+                low, high = fwd_press.at[spans[0], inside], fwd_press.at[spans[1], inside]
+            parts.append(Link(slot, x_pairs(low, high, plane, RIM)))
+            slot += 1
+        links_x.append(parts)
         parts = []
         for span, rows in zip(spans, inner):
 
@@ -287,7 +297,7 @@
         )
     )
     buoy_link = Link(slot, pairs)
-    links = [*links_x, *sum(links_y, []), *vel_links, buoy_link]
+    links = [*sum(links_x, []), *sum(links_y, []), *vel_links, buoy_link]
 
     for side in range(4):
 
@@ -317,9 +327,10 @@
 
     pl.semaphore_wait(barrier, greeted)
 
+    moves[0].wait()
     gathers = [
         remote(
-            latent_ref,
+            slabs.at[me],
             slabs.at[me],
             shot_send.at[0, d - 1],
             shot_recv.at[0, d - 1],
@@ -329,9 +340,9 @@
     ]
     for copy in gathers:
         copy.start()
-    for link in (links_x[0], *links_y[0], *vel_links):
+    for link in (*links_x[0], *links_y[0], *vel_links):
         link.send()
-    for move in moves:
+    for move in moves[1:]:
         move.wait()
 
     spread_rows = as_pick(one_hot((wide, CH), lambda r, c: r % CH == c))
@@ -353,7 +364,16 @@
         jnp.where(same_out, mm(mm(spread_rows, part).astype(half), order), 0.0).astype(half)
         for part in split(w_second[...])
     )
-    depth_pick = as_pick(one_hot((size_z, size_z), lambda r, c: 4 * (r % cells) + r // cells == c))
+    to_depth = as_pick(
+        one_hot((2 * size_z, size_z), lambda r, c: 4 * (r % cells) + r % size_z // cells == c)
+    )
+    from_depth = as_pick(
+        one_hot((2 * size_z, size_z), lambda r, c: 4 * (c % cells) + c // cells == r % size_z)
+    )
+
+    def side_by_side(values):
+        return jnp.concatenate(split(values), axis=1)
+
 
     count = rec_at.shape[2]
     local_x = rec_at[0] - me_x * size_x
@@ -408,29 +428,41 @@
     depth_c = slabs.shape[2]
     for s in range(shots):
         for a in range(rows_a):
-            latents[pl.ds(a * cells + s * depth_c, depth_c)] = slabs[s, a]
-    for h in range(halves):
-        lanes = slice(h * wide, (h + 1) * wide)
-        state = jnp.tanh(mm3(split(latents[:, lanes]), big_first))
-        hidden[:, lanes] = state
-        outputs = mm3(split(state), big_second)
-        for a in range(rows_a):
-            rows = slice(a * cells, (a + 1) * cells)
-            stacked = jnp.concatenate(
-                [outputs[rows, k * block : (k + 1) * block] for k in range(4)], axis=0
+            for h in range(halves):
+                latents[pl.ds((h * rows_a + a) * cells + s * depth_c, depth_c)] = slabs[
+                    s, a, :, h * wide : (h + 1) * wide
+                ]
+    hidden[...] = jnp.tanh(mm3(split(latents[...]), big_first))
+    outputs = mm3(split(hidden[...]), big_second)
+    blocks = [(h, a) for h in range(halves) for a in range(rows_a)]
+    stacked = jnp.concatenate(
+        [
+            jnp.transpose(
+                jnp.concatenate(
+                    [
+                        outputs[n * cells : (n + 1) * cells, k * block : (k + 1) * block]
+                        for k in range(4)
+                    ],
+                    axis=0,
+                )
             )
-            sig = logistic(mm2(split(jnp.transpose(stacked)), depth_pick))
-            gates[h, a] = sig
-            speed = 0.15 + 0.25 * sig[: block // 2]
-            density = 1.0 + 1.5 * sig[block // 2 :]
-            modulus = density * speed * speed
-            buoyancy = 1.0 / density
-            deep_y = 4 * GROUP
-            for i in range(4):
-                part = slice(i * deep_y, (i + 1) * deep_y)
-                mod[4 * a + i, pl.ds(h * deep_y, deep_y)] = modulus[part]
-                buoy_x[VRIM + 4 * a + i, pl.ds(h * deep_y, deep_y)] = buoyancy[part]
-                buoy_y[4 * a + i, pl.ds(VRIM + h * deep_y, deep_y)] = buoyancy[part]
+            for n in range(len(blocks))
+        ],
+        axis=0,
+    )
+    gates[...] = logistic(mm(side_by_side(stacked), to_depth)).reshape(gates.shape)
+    deep_y = 4 * GROUP
+    for n, (h, a) in enumerate(blocks):
+        sig = gates[n]
+        speed = 0.15 + 0.25 * sig[: block // 2]
+        density = 1.0 + 1.5 * sig[block // 2 :]
+        modulus = density * speed * speed
+        buoyancy = 1.0 / density
+        for i in range(4):
+            part = slice(i * deep_y, (i + 1) * deep_y)
+            mod[4 * a + i, pl.ds(h * deep_y, deep_y)] = modulus[part]
+            buoy_x[VRIM + 4 * a + i, pl.ds(h * deep_y, deep_y)] = buoyancy[part]
+            buoy_y[4 * a + i, pl.ds(VRIM + h * deep_y, deep_y)] = buoyancy[part]
     buoy_link.send()
 
     along = [
@@ -473,7 +505,7 @@
         vel_z[way] = moved
         diverge_z[...] = along_z(moved, tables[1])
 
-    def faces_x(state, way, moment, first, last):
+    def faces_x(state, way, moment, first, last, span):
         def one(c, carry):
             here, there = column_of(c, 0), column_of(c, PAD)
             rows = {
@@ -488,7 +520,7 @@
                     slope_x[moment, x, here] = slope
             return carry
 
-        lax.fori_loop(0, columns, one, 0)
+        lax.fori_loop(*span, one, 0)
 
     def faces_y(state, way, moment, rows):
         def one(x, carry):
@@ -503,7 +535,7 @@
 
         lax.fori_loop(rows[0], rows[1], one, 0, unroll=2)
 
-    def finish(state, way, moment, rows):
+    def finish(state, way, moment, rows, span):
         first, last = rows
 
         def one(c, carry):
@@ -549,11 +581,14 @@
                         press[state + 1, x + RIM, there] = value + misfit[moment - 1, x, here]
             return carry
 
-        lax.fori_loop(0, columns, one, 0)
+        lax.fori_loop(*span, one, 0)
+
+    every = (0, columns)
+    pieces = [(n * columns // PARTS, (n + 1) * columns // PARTS) for n in range(PARTS)]
 
     def step(state, way, moment):
         depth_part(state, way, moment)
-        faces_x(state, way, moment, 3, size_x - 4)
+        faces_x(state, way, moment, 3, size_x - 4, every)
         if state == 0:
             buoy_link.receive()
         if state % STEPS == 0:
@@ -563,17 +598,19 @@
             ends.reverse()
         more = state + 1 < 2 * STEPS
         for side, rows, ghosts in ends:
-            links_x[state].receive(side)
             links_y[state][side].receive()
-            faces_x(state, way, moment, *ghosts)
             faces_y(state, way, moment, rows)
-            finish(state, way, moment, rows)
+            for part, span in enumerate(pieces):
+                links_x[state][part].receive(side)
+                faces_x(state, way, moment, *ghosts, span)
+                finish(state, way, moment, rows, span)
+                if more:
+                    links_x[state + 1][part].send(side)
             if more:
-                links_x[state + 1].send(side)
                 links_y[state + 1][side].send()
         links_y[state][2].receive()
         faces_y(state, way, moment, mid_rows)
-        finish(state, way, moment, mid_rows)
+        finish(state, way, moment, mid_rows, every)
         if more:
             links_y[state + 1][2].send()
 
@@ -582,60 +619,31 @@
     for turn in range(STEPS):
         step(STEPS + turn, 1, STEPS - 1 - turn)
 
-    for h in range(halves):
-        for a in range(rows_a):
-            sig = gates[h, a]
-            deep_y = 4 * GROUP
-            here = pl.ds(h * deep_y, deep_y)
-            grad_mod = jnp.concatenate([totals[0, 4 * a + i, here] for i in range(4)], axis=0)
-            grad_buoy = jnp.concatenate([totals[1, 4 * a + i, here] for i in range(4)], axis=0)
-            sig_speed, sig_dens = sig[: block // 2], sig[block // 2 :]
-            speed = 0.15 + 0.25 * sig_speed
-            density = 1.0 + 1.5 * sig_dens
-            grad_speed = grad_mod * 2.0 * density * speed
-            grad_dens = grad_mod * speed * speed - grad_buoy / (density * density)
-            fine = jnp.concatenate(
-                [
-                    grad_speed * 0.25 * sig_speed * (1.0 - sig_speed),
-                    grad_dens * 1.5 * sig_dens * (1.0 - sig_dens),
-                ],
-                axis=0,
-            )
-            rows = jnp.transpose(mm2(split(fine), depth_pick, rows_by_rows))
-            for k in range(4):
-                turned[h, pl.ds(a * cells, cells), k * block : (k + 1) * block] = rows[
-                    k * cells : (k + 1) * cells
-                ]
-    big_gf = 0.0
-    big_gs = 0.0
-    scatters = []
-    for h in range(halves):
-        lanes = slice(h * wide, (h + 1) * wide)
-        state = hidden[:, lanes]
-        outer = split(turned[h])
-        grad_pre = mm3(outer, big_second, rows_by_rows) * (1.0 - state * state)
-        inner = split(grad_pre)
-        grad_rows = mm3(inner, big_first, rows_by_rows)
-        for s in range(shots):
-            for a in range(rows_a):
-                first = a * cells + s * depth_c
-                share[s, a, :, lanes] = grad_rows[first : first + depth_c]
-        for d in range(1, shots):
-            there = axis_peers("shot", d)
-            window = pl.ds(h * wide, wide)
-            copy = remote(
-                share.at[there["shot"], :, :, window],
-                landed.at[me, :, :, window],
-                shot_send.at[1 + h, d - 1],
-                shot_recv.at[1 + h, d - 1],
-                there,
-            )
-            copy.start()
-            scatters.append(copy)
-        big_gf = big_gf + mm3(split(jnp.transpose(latents[:, lanes])), inner)
-        big_gs = big_gs + mm3(split(jnp.transpose(state)), outer)
-    landed[me] = share[me]
-
+    for n, (h, a) in enumerate(blocks):
+        sig = gates[n]
+        here = pl.ds(h * deep_y, deep_y)
+        grad_mod = jnp.concatenate([totals[0, 4 * a + i, here] for i in range(4)], axis=0)
+        grad_buoy = jnp.concatenate([totals[1, 4 * a + i, here] for i in range(4)], axis=0)
+        sig_speed, sig_dens = sig[: block // 2], sig[block // 2 :]
+        speed = 0.15 + 0.25 * sig_speed
+        density = 1.0 + 1.5 * sig_dens
+        grad_speed = grad_mod * 2.0 * density * speed
+        grad_dens = grad_mod * speed * speed - grad_buoy / (density * density)
+        gates[n, pl.ds(0, block // 2)] = grad_speed * 0.25 * sig_speed * (1.0 - sig_speed)
+        gates[n, pl.ds(block // 2, block // 2)] = grad_dens * 1.5 * sig_dens * (1.0 - sig_dens)
+    permuted = mm(side_by_side(gates[...].reshape(len(blocks) * block, size_z)), from_depth)
+    for n in range(len(blocks)):
+        rows = jnp.transpose(permuted[n * block : (n + 1) * block])
+        for k in range(4):
+            turned[pl.ds(n * cells, cells), k * block : (k + 1) * block] = rows[
+                k * cells : (k + 1) * cells
+            ]
+    outer = split(turned[...])
+    inner = split(
+        mm3(outer, big_second, rows_by_rows) * (1.0 - hidden[...] * hidden[...])
+    )
+    big_gf = mm3(split(jnp.transpose(latents[...])), inner)
+    big_gs = mm3(split(jnp.transpose(hidden[...])), outer)
     sum_f = 0.0
     sum_s = 0.0
     for b in range(GROUP):
@@ -654,9 +662,6 @@
             split(sum_f[side * CH // 2 : (side + 1) * CH // 2]), fold
         )
     weights = jnp.concatenate([grad_second, grad_first], axis=0)
-    piece = weights.shape[0] // shots
-    for s in range(shots):
-        w_share[s] = weights[s * piece : (s + 1) * piece]
 
     def total(stack):
         summed = stack[0]
@@ -664,48 +669,93 @@
             summed = summed + stack[n]
         return summed
 
-    hops = [
+    peers = list(plane_peers())
+    tiles = len(peers) + 1
+    spot = me_x * lax.axis_size("gy") + me_y
+    piece = weights.shape[0] // tiles
+    for n in range(tiles):
+        w_share[n] = weights[n * piece : (n + 1) * piece]
+    first_hops = [
         remote(
-            w_share.at[axis_peers("shot", d)["shot"]],
-            w_landed.at[me],
-            shot_send.at[1 + halves, d - 1],
-            shot_recv.at[1 + halves, d - 1],
+            w_share.at[peer["gx"] * lax.axis_size("gy") + peer["gy"]],
+            w_landed.at[spot],
+            plane_send.at[0, n],
+            plane_recv.at[0, n],
+            peer,
+        )
+        for n, peer in enumerate(peers)
+    ]
+    for hop in first_hops:
+        hop.start()
+    w_landed[spot] = w_share[spot]
+
+    grad_rows = mm3(inner, big_first, rows_by_rows)
+    for n, (h, a) in enumerate(blocks):
+        for s in range(shots):
+            first = n * cells + s * depth_c
+            share[s % 2, s // 2, a, :, h * wide : (h + 1) * wide] = grad_rows[
+                first : first + depth_c
+            ]
+    mate = lax.rem(me, 2)
+    group = me // 2
+    other = 1 - mate
+    swap = remote(
+        share.at[other],
+        paired,
+        shot_send.at[1, 0],
+        shot_recv.at[1, 0],
+        {"shot": 2 * group + other},
+    )
+    swap.start()
+    for hop in first_hops:
+        hop.wait()
+    w_plane[me] = total(w_landed)
+    second_hops = [
+        remote(
+            w_plane.at[me],
+            w_plane.at[me],
+            shot_send.at[2, d - 1],
+            shot_recv.at[2, d - 1],
             axis_peers("shot", d),
         )
         for d in range(1, shots)
     ]
-    for hop in hops:
+    for hop in second_hops:
         hop.start()
-    w_landed[me] = w_share[me]
-    for hop in hops:
+    swap.wait()
+    groups = shots // 2
+    for g in range(groups):
+        summed[g] = share[mate, g] + paired[g]
+    scatters = []
+    for d in range(1, groups):
+        there = lax.rem(group + d, groups)
+        scatters.append(
+            remote(
+                summed.at[there],
+                landed.at[group],
+                shot_send.at[3, d - 1],
+                shot_recv.at[3, d - 1],
+                {"shot": 2 * there + mate},
+            )
+        )
+    for copy in scatters:
+        copy.start()
+    landed[group] = summed[group]
+    for hop in second_hops:
         hop.wait()
-    spot = me_x * lax.axis_size("gy") + me_y
-    w_plane[spot] = total(w_landed)
-    hops = [
-        remote(w_plane.at[spot], w_plane.at[spot], plane_send.at[n], plane_recv.at[n], peer)
-        for n, peer in enumerate(plane_peers())
+    sums_ref[spot] = total(w_plane)
+    third_hops = [
+        remote(
+            sums_ref.at[spot], sums_ref.at[spot], plane_send.at[1, n], plane_recv.at[1, n], peer
+        )
+        for n, peer in enumerate(peers)
     ]
-    for hop in hops:
-        hop.start()
-    for hop in hops:
-        hop.wait()
-    sums_ref[me] = total(w_plane)
-    hops = [
-        remote(
-            sums_ref.at[me],
-            sums_ref.at[me],
-            shot_send.at[2 + halves, d - 1],
-            shot_recv.at[2 + halves, d - 1],
-            axis_peers("shot", d),
-        )
-        for d in range(1, shots)
-    ]
-    for hop in hops:
+    for hop in third_hops:
         hop.start()
     for copy in scatters:
         copy.wait()
     own_ref[...] = total(landed)
-    for hop in hops:
+    for hop in third_hops:
         hop.wait()
     for link in links:
         link.sent()
@@ -761,8 +811,8 @@
     count = rec_pos.shape[2]
     anywhere = pl.BlockSpec(memory_space=pl.ANY)
     vmem = pl.BlockSpec(memory_space=pltpu.VMEM)
-    slots = 4 * 2 * STEPS + 3
-    piece = (CH + CH // 2) // shots
+    slots = (3 + PARTS) * 2 * STEPS + 3
+    piece = (CH + CH // 2) // tiles
 
     def scratch(*shape, kind=jnp.float32):
         return pltpu.VMEM(shape, kind)
@@ -774,7 +824,7 @@
         whole_kernel,
         out_shape=(
             jax.ShapeDtypeStruct((rows_a, depth_c, merged), jnp.float32),
-            jax.ShapeDtypeStruct((shots, piece, outs), jnp.float32),
+            jax.ShapeDtypeStruct((tiles, piece, outs), jnp.float32),
         ),
         in_specs=[anywhere] * 11,
         out_specs=(vmem, vmem),
@@ -787,9 +837,9 @@
             scratch(STEPS, 1, count),
             scratch(*field),
             scratch(shots, rows_a, depth_c, merged),
-            scratch(rows_a * cells, merged),
-            scratch(rows_a * cells, merged),
-            scratch(halves, rows_a, GROUP * outs // 4, size_z),
+            scratch(halves * rows_a * cells, GROUP * CH),
+            scratch(halves * rows_a * cells, GROUP * CH),
+            scratch(halves * rows_a, GROUP * outs // 4, size_z),
             scratch(*field),
             scratch(STEPS, *field),
             scratch((2 * STEPS + 1) * size_z, count, kind=half),
@@ -808,19 +858,21 @@
             scratch(STEPS, size_x, size_y + 2 * VRIM, size_z),
             scratch(STEPS, *field),
             scratch(2, *field),
-            scratch(halves, rows_a * cells, GROUP * outs),
-            scratch(shots, rows_a, depth_c, merged),
-            scratch(shots, rows_a, depth_c, merged),
+            scratch(halves * rows_a * cells, GROUP * outs),
+            scratch(2, shots // 2, rows_a, depth_c, merged),
+            scratch(shots // 2, rows_a, depth_c, merged),
+            scratch(shots // 2, rows_a, depth_c, merged),
+            scratch(shots // 2, rows_a, depth_c, merged),
+            scratch(tiles, piece, outs),
+            scratch(tiles, piece, outs),
             scratch(shots, piece, outs),
-            scratch(shots, piece, outs),
-            scratch(tiles, piece, outs),
             sems(15),
             sems(slots, 4),
             sems(slots, 4),
-            sems(3 + halves, shots),
-            sems(3 + halves, shots),
-            sems(tiles),
-            sems(tiles),
+            sems(4, shots),
+            sems(4, shots),
+            sems(2, tiles),
+            sems(2, tiles),
         ],
         compiler_params=pltpu.CompilerParams(
             collective_id=0, has_side_effects=True, vmem_limit_bytes=60 * 1024 * 1024
@@ -845,7 +897,7 @@
             jax.ShapeDtypeStruct(w_first.shape, jnp.float32),
             jax.ShapeDtypeStruct(w_second.shape, jnp.float32),
         ),
-        scratch_shapes=[scratch(shots * piece, outs)],
+        scratch_shapes=[scratch(tiles * piece, outs)],
     )(own, sums)
     return grad_latent.transpose(1, 0, 2), grad_first, grad_second
 

time: 61.1 us -> 60.3 us (0.987)
  Pallas kernels: 60.3 us -> 59.5 us
    pallas_call x1, Pallas kernels: 58.7 us -> 57.9 us  [body(): pl.pallas_call(whole_kernel, out_shape=(jax.ShapeDtypeStruct((rows_a, dep...]
where the time goes in v3:
time: 60.3 us; the launch traced here: 60.1 us
  Pallas kernels  59.5 us (99%)
  between operations  0.64 us (1%)
    pallas_call x1, Pallas kernels, body(): pl.pallas_call(whole_kernel, out_shape=(jax.ShapeDtypeStruct((rows_a, dep...  57.9 us
    pallas_call x1, Pallas kernels, body(): pl.pallas_call(finish_kernel, out_shape=(jax.ShapeDtypeStruct(own.shape,...  1.6 us

profile of v3, /device:TPU:0, one launch (start us, length us, event | category | flops | bytes accessed | tf_op | source)
XLA Modules:
  0.0 60.1 jit_solution(11740848327339755846)
XLA Ops:
  0.6 57.9 %shard_map.130 = (f32[6,8,512]{2,1,0:T(8,128)}, f32[8,12,128]{2,1,0:T(8,128)}) custom-call(f32[6,8,512]{2,1,0:T(8,128)} %bitcast.14, f32[64,64]{1,0:T(8,128)} %first_ref.1, f32[64,128]{1,0:T(8,128)} %second_ref.1, f32[24,32,128]{2,1,0:T(8,128)} %bitcast.12, f32[3,24,32,128]{3,2,1,0:T(8,128)} %bitcast.10, f32[24,32,128]{2,1,0:T(8,128)} %bitcast.13, ...), custom_call_target="tpu_custom_call" | custom-call | tf_op jit(solution)/shard_map/pallas_call | solution.py:823
  58.5 1.6 %shard_map.131 = (f32[6,8,512]{2,1,0:T(8,128)}, f32[64,64]{1,0:T(8,128)}, f32[64,128]{1,0:T(8,128)}) custom-call(f32[6,8,512]{2,1,0:T(8,128)} %get-tuple-element.8.own_ref, f32[8,12,128]{2,1,0:T(8,128)} %get-tuple-element.9.sums_ref), custom_call_target="tpu_custom_call" | custom-call | tf_op jit(solution)/shard_map/pallas_call | solution.py:893

commit v4 on v3

--- a/solution.py
+++ b/solution.py
@@ -44,6 +44,16 @@
     rows = lax.broadcasted_iota(jnp.int32, shape, 0)
     cols = lax.broadcasted_iota(jnp.int32, shape, 1)
     return rule(rows, cols)
+
+
+def low_part(values, size):
+    assert size & (size - 1) == 0
+    return values & (size - 1)
+
+
+def high_part(values, size):
+    assert size & (size - 1) == 0
+    return values >> (size.bit_length() - 1)
 
 
 def as_pick(mask):
@@ -124,7 +134,6 @@
     vel_y,
     vel_z,
     diverge_z,
-    misfit,
     div_at,
     slope_x,
     slope_y,
@@ -141,6 +150,8 @@
     local_sem,
     send_sem,
     recv_sem,
+    gather_send,
+    gather_recv,
     shot_send,
     shot_recv,
     plane_send,
@@ -328,25 +339,36 @@
     pl.semaphore_wait(barrier, greeted)
 
     moves[0].wait()
-    gathers = [
-        remote(
-            slabs.at[me],
-            slabs.at[me],
-            shot_send.at[0, d - 1],
-            shot_recv.at[0, d - 1],
-            axis_peers("shot", d),
-        )
-        for d in range(1, shots)
-    ]
-    for copy in gathers:
+    mate = lax.rem(me, 2)
+    group = me // 2
+    groups = shots // 2
+    other_core = {"shot": 2 * group + 1 - mate}
+    cut = rows_a // 2
+    layers_of = (pl.ds(0, cut), pl.ds(cut, rows_a - cut))
+
+    def pass_on(owner, part, peer, row, column):
+        rows = slabs.at[owner, layers_of[part]]
+        return remote(
+            rows, rows, gather_send.at[part, row, column], gather_recv.at[part, row, column], peer
+        )
+
+    afar, passed = [], []
+    for part in range(2):
+        for d in range(1, groups):
+            there = {"shot": 2 * lax.rem(group + d, groups) + mate}
+            afar.append(pass_on(me, part, there, 0, d))
+            owner = 2 * lax.rem(group - d + groups, groups) + mate
+            passed.append(pass_on(owner, part, other_core, 1, d))
+    beside = [pass_on(me, part, other_core, 1, 0) for part in range(2)]
+    for copy in afar + beside:
         copy.start()
     for link in (*links_x[0], *links_y[0], *vel_links):
         link.send()
     for move in moves[1:]:
         move.wait()
 
-    spread_rows = as_pick(one_hot((wide, CH), lambda r, c: r % CH == c))
-    same_cell = one_hot((wide, wide), lambda r, c: r // CH == c // CH)
+    spread_rows = as_pick(one_hot((wide, CH), lambda r, c: low_part(r, CH) == c))
+    same_cell = one_hot((wide, wide), lambda r, c: high_part(r, CH) == high_part(c, CH))
     big_first = tuple(
         jnp.where(same_cell, mm(mm(spread_rows, part).astype(half), spread_rows, rows_by_rows), 0.0)
         .astype(half)
@@ -356,19 +378,19 @@
     block = outs // 4 * GROUP
 
     def source_of(c):
-        return c % block // 64 * 64 + c % 64 // 16 * 16 + c % 4 * 4 + c // block
+        return (c & (block - 16)) + 4 * low_part(c, 4) + high_part(c, block)
 
     order = as_pick(one_hot((outs, 4 * block), lambda r, c: source_of(c) == r))
-    same_out = one_hot((wide, 4 * block), lambda r, c: c % 16 // 4 == r // CH)
+    same_out = one_hot((wide, 4 * block), lambda r, c: high_part(c & 12, 4) == high_part(r, CH))
     big_second = tuple(
         jnp.where(same_out, mm(mm(spread_rows, part).astype(half), order), 0.0).astype(half)
         for part in split(w_second[...])
     )
     to_depth = as_pick(
-        one_hot((2 * size_z, size_z), lambda r, c: 4 * (r % cells) + r % size_z // cells == c)
+        one_hot((2 * size_z, size_z), lambda r, c: 4 * low_part(r, cells) + high_part(low_part(r, size_z), cells) == c)
     )
     from_depth = as_pick(
-        one_hot((2 * size_z, size_z), lambda r, c: 4 * (c % cells) + c // cells == r % size_z)
+        one_hot((2 * size_z, size_z), lambda r, c: 4 * low_part(c, cells) + high_part(c, cells) == low_part(r, size_z))
     )
 
     def side_by_side(values):
@@ -407,7 +429,6 @@
             )
         return carry
 
-    lax.fori_loop(0, size_x // chunk, planes, 0)
 
     src_x = place[:, 0:1] - me_x * size_x
     src_y = place[:, 1:2] - me_y * size_y
@@ -423,8 +444,11 @@
 
     lax.fori_loop(0, size_x, kick, 0)
 
-    for copy in gathers:
-        copy.wait()
+    for arriving, forward in zip(afar, passed):
+        arriving.wait_recv()
+        forward.start()
+    for copy in beside + passed:
+        copy.wait_recv()
     depth_c = slabs.shape[2]
     for s in range(shots):
         for a in range(rows_a):
@@ -557,13 +581,11 @@
                 value = press[state, x + RIM, there] - mod[x, here] * div
                 if way == 0:
                     value = value + kicks[moment, x, here]
-                    residue = hits[x, here] * value - recorded[moment, x, here]
                     div_at[moment, x, here] = div
                     if moment == STEPS - 1:
-                        press[state + 1, x + RIM, there] = start_adj[x, here] + residue
-                    else:
-                        misfit[moment, x, here] = residue
-                        press[state + 1, x + RIM, there] = value
+                        residue = hits[x, here] * value - recorded[moment, x, here]
+                        value = start_adj[x, here] + residue
+                    press[state + 1, x + RIM, there] = value
                 else:
                     part_mod = value * div_at[moment, x, here]
                     part_buoy = (
@@ -578,7 +600,9 @@
                         totals[0, x, here] = totals[0, x, here] - part_mod
                         totals[1, x, here] = totals[1, x, here] - part_buoy
                     if moment > 0:
-                        press[state + 1, x + RIM, there] = value + misfit[moment - 1, x, here]
+                        modelled = press[moment, x + RIM, there]
+                        residue = hits[x, here] * modelled - recorded[moment - 1, x, here]
+                        press[state + 1, x + RIM, there] = value + residue
             return carry
 
         lax.fori_loop(*span, one, 0)
@@ -589,6 +613,9 @@
     def step(state, way, moment):
         depth_part(state, way, moment)
         faces_x(state, way, moment, 3, size_x - 4, every)
+        if state < STEPS:
+            turns = size_x // chunk
+            lax.fori_loop(state * turns // STEPS, (state + 1) * turns // STEPS, planes, 0)
         if state == 0:
             buoy_link.receive()
         if state % STEPS == 0:
@@ -649,15 +676,15 @@
     for b in range(GROUP):
         mine = slice(b * CH, (b + 1) * CH)
         sum_f = sum_f + jnp.where(
-            one_hot((CH, wide), lambda r, c: c // CH == b), big_gf[mine], 0.0
+            one_hot((CH, wide), lambda r, c: high_part(c, CH) == b), big_gf[mine], 0.0
         )
         sum_s = sum_s + jnp.where(
-            one_hot((CH, 4 * block), lambda r, c: c % 16 // 4 == b), big_gs[mine], 0.0
+            one_hot((CH, 4 * block), lambda r, c: high_part(c & 12, 4) == b), big_gs[mine], 0.0
         )
     grad_second = mm2(split(sum_s), order, rows_by_rows)
     grad_first = 0.0
     for side in range(2):
-        fold = as_pick(one_hot((wide, outs), lambda r, c: r % CH + side * CH == c))
+        fold = as_pick(one_hot((wide, outs), lambda r, c: low_part(r, CH) + side * CH == c))
         grad_first = grad_first + mm2(
             split(sum_f[side * CH // 2 : (side + 1) * CH // 2]), fold
         )
@@ -670,24 +697,23 @@
         return summed
 
     peers = list(plane_peers())
-    tiles = len(peers) + 1
     spot = me_x * lax.axis_size("gy") + me_y
-    piece = weights.shape[0] // tiles
-    for n in range(tiles):
+    piece = weights.shape[0] // shots
+    for n in range(shots):
         w_share[n] = weights[n * piece : (n + 1) * piece]
     first_hops = [
         remote(
-            w_share.at[peer["gx"] * lax.axis_size("gy") + peer["gy"]],
-            w_landed.at[spot],
-            plane_send.at[0, n],
-            plane_recv.at[0, n],
-            peer,
-        )
-        for n, peer in enumerate(peers)
+            w_share.at[axis_peers("shot", d)["shot"]],
+            w_landed.at[me],
+            shot_send.at[0, d - 1],
+            shot_recv.at[0, d - 1],
+            axis_peers("shot", d),
+        )
+        for d in range(1, shots)
     ]
     for hop in first_hops:
         hop.start()
-    w_landed[spot] = w_share[spot]
+    w_landed[me] = w_share[me]
 
     grad_rows = mm3(inner, big_first, rows_by_rows)
     for n, (h, a) in enumerate(blocks):
@@ -696,34 +722,24 @@
             share[s % 2, s // 2, a, :, h * wide : (h + 1) * wide] = grad_rows[
                 first : first + depth_c
             ]
-    mate = lax.rem(me, 2)
-    group = me // 2
-    other = 1 - mate
     swap = remote(
-        share.at[other],
+        share.at[1 - mate],
         paired,
         shot_send.at[1, 0],
         shot_recv.at[1, 0],
-        {"shot": 2 * group + other},
+        other_core,
     )
     swap.start()
     for hop in first_hops:
         hop.wait()
-    w_plane[me] = total(w_landed)
+    w_plane[spot] = total(w_landed)
     second_hops = [
-        remote(
-            w_plane.at[me],
-            w_plane.at[me],
-            shot_send.at[2, d - 1],
-            shot_recv.at[2, d - 1],
-            axis_peers("shot", d),
-        )
-        for d in range(1, shots)
+        remote(w_plane.at[spot], w_plane.at[spot], plane_send.at[n], plane_recv.at[n], peer)
+        for n, peer in enumerate(peers)
     ]
     for hop in second_hops:
         hop.start()
     swap.wait()
-    groups = shots // 2
     for g in range(groups):
         summed[g] = share[mate, g] + paired[g]
     scatters = []
@@ -743,12 +759,16 @@
     landed[group] = summed[group]
     for hop in second_hops:
         hop.wait()
-    sums_ref[spot] = total(w_plane)
+    sums_ref[me] = total(w_plane)
     third_hops = [
         remote(
-            sums_ref.at[spot], sums_ref.at[spot], plane_send.at[1, n], plane_recv.at[1, n], peer
-        )
-        for n, peer in enumerate(peers)
+            sums_ref.at[me],
+            sums_ref.at[me],
+            shot_send.at[4, d - 1],
+            shot_recv.at[4, d - 1],
+            axis_peers("shot", d),
+        )
+        for d in range(1, shots)
     ]
     for hop in third_hops:
         hop.start()
@@ -757,6 +777,8 @@
     own_ref[...] = total(landed)
     for hop in third_hops:
         hop.wait()
+    for copy in afar + beside + passed:
+        copy.wait_send()
     for link in links:
         link.sent()
 
@@ -812,7 +834,7 @@
     anywhere = pl.BlockSpec(memory_space=pl.ANY)
     vmem = pl.BlockSpec(memory_space=pltpu.VMEM)
     slots = (3 + PARTS) * 2 * STEPS + 3
-    piece = (CH + CH // 2) // tiles
+    piece = (CH + CH // 2) // shots
 
     def scratch(*shape, kind=jnp.float32):
         return pltpu.VMEM(shape, kind)
@@ -824,7 +846,7 @@
         whole_kernel,
         out_shape=(
             jax.ShapeDtypeStruct((rows_a, depth_c, merged), jnp.float32),
-            jax.ShapeDtypeStruct((tiles, piece, outs), jnp.float32),
+            jax.ShapeDtypeStruct((shots, piece, outs), jnp.float32),
         ),
         in_specs=[anywhere] * 11,
         out_specs=(vmem, vmem),
@@ -852,7 +874,6 @@
             scratch(2, size_x, size_y + 2 * VRIM, size_z),
             scratch(2, *field),
             scratch(*field),
-            scratch(STEPS - 1, *field),
             scratch(STEPS, *field),
             scratch(STEPS, *field),
             scratch(STEPS, size_x, size_y + 2 * VRIM, size_z),
@@ -863,16 +884,18 @@
             scratch(shots // 2, rows_a, depth_c, merged),
             scratch(shots // 2, rows_a, depth_c, merged),
             scratch(shots // 2, rows_a, depth_c, merged),
+            scratch(shots, piece, outs),
+            scratch(shots, piece, outs),
             scratch(tiles, piece, outs),
-            scratch(tiles, piece, outs),
-            scratch(shots, piece, outs),
             sems(15),
             sems(slots, 4),
             sems(slots, 4),
-            sems(4, shots),
-            sems(4, shots),
-            sems(2, tiles),
-            sems(2, tiles),
+            sems(2, 2, shots // 2),
+            sems(2, 2, shots // 2),
+            sems(5, shots),
+            sems(5, shots),
+            sems(tiles),
+            sems(tiles),
         ],
         compiler_params=pltpu.CompilerParams(
             collective_id=0, has_side_effects=True, vmem_limit_bytes=60 * 1024 * 1024
@@ -897,7 +920,7 @@
             jax.ShapeDtypeStruct(w_first.shape, jnp.float32),
             jax.ShapeDtypeStruct(w_second.shape, jnp.float32),
         ),
-        scratch_shapes=[scratch(tiles * piece, outs)],
+        scratch_shapes=[scratch(shots * piece, outs)],
     )(own, sums)
     return grad_latent.transpose(1, 0, 2), grad_first, grad_second
 

time: 60.3 us -> 55.6 us (0.922)
  Pallas kernels: 59.5 us -> 54.8 us
    pallas_call x1, Pallas kernels: 57.9 us -> 53.2 us  [body(): pl.pallas_call(whole_kernel, out_shape=(jax.ShapeDtypeStruct((rows_a, dep...]
where the time goes in v4:
time: 55.6 us; the launch traced here: 55.4 us
  Pallas kernels  54.8 us (99%)
  between operations  0.64 us (1%)
    pallas_call x1, Pallas kernels, body(): pl.pallas_call(whole_kernel, out_shape=(jax.ShapeDtypeStruct((rows_a, dep...  53.2 us
    pallas_call x1, Pallas kernels, body(): pl.pallas_call(finish_kernel, out_shape=(jax.ShapeDtypeStruct(own.shape,...  1.59 us

profile of v4, /device:TPU:0, one launch (start us, length us, event | category | flops | bytes accessed | tf_op | source)
XLA Modules:
  0.0 55.4 jit_solution(3228315267474913058)
XLA Ops:
  0.6 53.2 %shard_map.130 = (f32[6,8,512]{2,1,0:T(8,128)}, f32[4,24,128]{2,1,0:T(8,128)}) custom-call(f32[6,8,512]{2,1,0:T(8,128)} %bitcast.14, f32[64,64]{1,0:T(8,128)} %first_ref.1, f32[64,128]{1,0:T(8,128)} %second_ref.1, f32[24,32,128]{2,1,0:T(8,128)} %bitcast.12, f32[3,24,32,128]{3,2,1,0:T(8,128)} %bitcast.10, f32[24,32,128]{2,1,0:T(8,128)} %bitcast.13, ...), custom_call_target="tpu_custom_call" | custom-call | tf_op jit(solution)/shard_map/pallas_call | solution.py:845
  53.8 1.6 %shard_map.131 = (f32[6,8,512]{2,1,0:T(8,128)}, f32[64,64]{1,0:T(8,128)}, f32[64,128]{1,0:T(8,128)}) custom-call(f32[6,8,512]{2,1,0:T(8,128)} %get-tuple-element.8.own_ref, f32[4,24,128]{2,1,0:T(8,128)} %get-tuple-element.9.sums_ref), custom_call_target="tpu_custom_call" | custom-call | tf_op jit(solution)/shard_map/pallas_call | solution.py:916

commit v5 on v4

--- a/solution.py
+++ b/solution.py
@@ -11,7 +11,6 @@
 VRIM = 4
 PAD = 8
 GROUP = 4
-PARTS = 2
 LANES = 128
 
 coeffs = (1225.0 / 1024.0, -245.0 / 3072.0, 49.0 / 5120.0, -5.0 / 7168.0)
@@ -122,6 +121,8 @@
     latents,
     hidden,
     gates,
+    factors,
+    across,
     hits,
     recorded,
     rec_weights,
@@ -237,18 +238,15 @@
 
     slot = 0
     links_x, links_y = [], []
-    deep_part = size_y // PARTS
     spans = (pl.ds(0, RIM), pl.ds(size_x - RIM, RIM), pl.ds(RIM, size_x - 2 * RIM))
     inner = (pl.ds(RIM, RIM), pl.ds(size_x, RIM), pl.ds(2 * RIM, size_x - 2 * RIM))
     for state in range(2 * STEPS):
         parts = []
-        for part in range(PARTS):
-            inside = pl.ds(part * deep_part, deep_part)
-
-            def plane(first, count, state=state, part=part):
-                return press.at[
-                    state, pl.ds(first, count), pl.ds(PAD + part * deep_part, deep_part)
-                ]
+        for at_y, deep in ((PAD, size_y - 2 * PAD), (0, PAD), (size_y - PAD, PAD)):
+            inside = pl.ds(at_y, deep)
+
+            def plane(first, count, state=state, at_y=at_y, deep=deep):
+                return press.at[state, pl.ds(first, count), pl.ds(PAD + at_y, deep)]
 
             low, high = plane(RIM, RIM), plane(size_x, RIM)
             if state == 0:
@@ -459,35 +457,44 @@
     hidden[...] = jnp.tanh(mm3(split(latents[...]), big_first))
     outputs = mm3(split(hidden[...]), big_second)
     blocks = [(h, a) for h in range(halves) for a in range(rows_a)]
-    stacked = jnp.concatenate(
-        [
-            jnp.transpose(
-                jnp.concatenate(
-                    [
-                        outputs[n * cells : (n + 1) * cells, k * block : (k + 1) * block]
-                        for k in range(4)
-                    ],
-                    axis=0,
+    deep_y = 4 * GROUP
+
+    def materials(group_of):
+        stacked = jnp.concatenate(
+            [
+                jnp.transpose(
+                    jnp.concatenate(
+                        [
+                            outputs[n * cells : (n + 1) * cells, k * block : (k + 1) * block]
+                            for k in range(4)
+                        ],
+                        axis=0,
+                    )
                 )
-            )
-            for n in range(len(blocks))
-        ],
-        axis=0,
-    )
-    gates[...] = logistic(mm(side_by_side(stacked), to_depth)).reshape(gates.shape)
-    deep_y = 4 * GROUP
-    for n, (h, a) in enumerate(blocks):
-        sig = gates[n]
-        speed = 0.15 + 0.25 * sig[: block // 2]
-        density = 1.0 + 1.5 * sig[block // 2 :]
-        modulus = density * speed * speed
-        buoyancy = 1.0 / density
-        for i in range(4):
-            part = slice(i * deep_y, (i + 1) * deep_y)
-            mod[4 * a + i, pl.ds(h * deep_y, deep_y)] = modulus[part]
-            buoy_x[VRIM + 4 * a + i, pl.ds(h * deep_y, deep_y)] = buoyancy[part]
-            buoy_y[4 * a + i, pl.ds(VRIM + h * deep_y, deep_y)] = buoyancy[part]
-    buoy_link.send()
+                for n in group_of
+            ],
+            axis=0,
+        )
+        sigs = logistic(mm(side_by_side(stacked), to_depth))
+        for at, n in enumerate(group_of):
+            h, a = blocks[n]
+            sig = sigs[at * block : (at + 1) * block]
+            gates[n] = sig
+            speed = 0.15 + 0.25 * sig[: block // 2]
+            density = 1.0 + 1.5 * sig[block // 2 :]
+            modulus = density * speed * speed
+            buoyancy = 1.0 / density
+            for i in range(4):
+                part = slice(i * deep_y, (i + 1) * deep_y)
+                mod[4 * a + i, pl.ds(h * deep_y, deep_y)] = modulus[part]
+                buoy_x[VRIM + 4 * a + i, pl.ds(h * deep_y, deep_y)] = buoyancy[part]
+                buoy_y[4 * a + i, pl.ds(VRIM + h * deep_y, deep_y)] = buoyancy[part]
+
+    at_ends = [n for n, (h, a) in enumerate(blocks) if a in (0, rows_a - 1)]
+    materials(at_ends)
+    buoy_link.send(0, 1)
+    materials([n for n in range(len(blocks)) if n not in at_ends])
+    buoy_link.send(2, 3)
 
     along = [
         split(matrix) for matrix in depth_matrices(size_z)
@@ -530,7 +537,8 @@
         diverge_z[...] = along_z(moved, tables[1])
 
     def faces_x(state, way, moment, first, last, span):
-        def one(c, carry):
+        def one(n, carry):
+            c = n * span[2]
             here, there = column_of(c, 0), column_of(c, PAD)
             rows = {
                 i: press[state, i + RIM, there] for i in range(first - 3, last + 4)
@@ -544,17 +552,20 @@
                     slope_x[moment, x, here] = slope
             return carry
 
-        lax.fori_loop(*span, one, 0)
-
-    def faces_y(state, way, moment, rows):
+        lax.fori_loop(span[0], span[1], one, 0)
+
+    def faces_y(state, way, moment, rows, strips_of):
         def one(x, carry):
-            def at(r):
-                return press[state, x + RIM, pl.ds(VRIM + r, size_y + 2 * VRIM)]
-
-            slope = weigh([at(r) for r in (1, 2, 3, 4)], [at(1 - r) for r in (1, 2, 3, 4)])
-            vel_y[way, x] = vel_y[way, x] - buoy_y[x] * slope
-            if way == 0:
-                slope_y[moment, x] = slope
+            for first, deep in strips_of:
+
+                def at(r):
+                    return press[state, x + RIM, pl.ds(VRIM + first + r, deep)]
+
+                here = pl.ds(first, deep)
+                slope = weigh([at(r) for r in (1, 2, 3, 4)], [at(1 - r) for r in (1, 2, 3, 4)])
+                vel_y[way, x, here] = vel_y[way, x, here] - buoy_y[x, here] * slope
+                if way == 0:
+                    slope_y[moment, x, here] = slope
             return carry
 
         lax.fori_loop(rows[0], rows[1], one, 0, unroll=2)
@@ -562,7 +573,8 @@
     def finish(state, way, moment, rows, span):
         first, last = rows
 
-        def one(c, carry):
+        def one(n, carry):
+            c = n * span[2]
             here, there = column_of(c, 0), column_of(c, PAD)
             speeds = {
                 i: vel_x[way, i + VRIM, here] for i in range(first - VRIM, last + VRIM - 1)
@@ -605,10 +617,29 @@
                         press[state + 1, x + RIM, there] = value + residue
             return carry
 
-        lax.fori_loop(*span, one, 0)
-
-    every = (0, columns)
-    pieces = [(n * columns // PARTS, (n + 1) * columns // PARTS) for n in range(PARTS)]
+        lax.fori_loop(span[0], span[1], one, 0)
+
+    def prepare_gates():
+        for n in range(len(blocks)):
+            sig = gates[n]
+            sig_speed, sig_dens = sig[: block // 2], sig[block // 2 :]
+            speed = 0.15 + 0.25 * sig_speed
+            density = 1.0 + 1.5 * sig_dens
+            inverse = 1.0 / density
+            bend = 1.5 * sig_dens * (1.0 - sig_dens)
+            factors[0, n] = 0.5 * density * speed * sig_speed * (1.0 - sig_speed)
+            factors[1, n] = speed * speed * bend
+            factors[2, n] = inverse * inverse * bend
+
+    def prepare_rows():
+        for n, rows in enumerate((latents, hidden)):
+            high, low = split(jnp.transpose(rows[...]))
+            across[n, 0] = high
+            across[n, 1] = low
+
+    every, inner_columns, outer_columns = (0, columns, 1), (1, columns - 1, 1), (0, 2, columns - 1)
+    inner_strips = ((8, size_y + 2 * VRIM - 16),)
+    outer_strips = ((0, 8), (size_y + 2 * VRIM - 8, 8))
 
     def step(state, way, moment):
         depth_part(state, way, moment)
@@ -616,28 +647,45 @@
         if state < STEPS:
             turns = size_x // chunk
             lax.fori_loop(state * turns // STEPS, (state + 1) * turns // STEPS, planes, 0)
-        if state == 0:
-            buoy_link.receive()
-        if state % STEPS == 0:
-            vel_links[way].receive()
         ends = [(0, low_rows, (-VRIM, 3)), (1, high_rows, (size_x - 4, size_x + 3))]
         if state % 2:
             ends.reverse()
         more = state + 1 < 2 * STEPS
+        if state == 0:
+            buoy_link.receive(0, 1)
+        if state % STEPS == 0:
+            vel_links[way].receive(0, 1)
+        for side, rows, ghosts in ends:
+            faces_y(state, way, moment, rows, inner_strips)
+            links_x[state][0].receive(side)
+            faces_x(state, way, moment, *ghosts, inner_columns)
+            finish(state, way, moment, rows, inner_columns)
+            if more:
+                links_x[state + 1][0].send(side)
+        faces_y(state, way, moment, mid_rows, inner_strips)
+        finish(state, way, moment, mid_rows, inner_columns)
+        if state == STEPS + 1:
+            prepare_gates()
+        if state == STEPS + 2:
+            prepare_rows()
+        if state == 0:
+            buoy_link.receive(2, 3)
+        if state % STEPS == 0:
+            vel_links[way].receive(2, 3)
         for side, rows, ghosts in ends:
             links_y[state][side].receive()
-            faces_y(state, way, moment, rows)
-            for part, span in enumerate(pieces):
+            for part in (1, 2):
                 links_x[state][part].receive(side)
-                faces_x(state, way, moment, *ghosts, span)
-                finish(state, way, moment, rows, span)
-                if more:
-                    links_x[state + 1][part].send(side)
+            faces_x(state, way, moment, *ghosts, outer_columns)
+            faces_y(state, way, moment, rows, outer_strips)
+            finish(state, way, moment, rows, outer_columns)
             if more:
                 links_y[state + 1][side].send()
+                for part in (1, 2):
+                    links_x[state + 1][part].send(side)
         links_y[state][2].receive()
-        faces_y(state, way, moment, mid_rows)
-        finish(state, way, moment, mid_rows, every)
+        faces_y(state, way, moment, mid_rows, outer_strips)
+        finish(state, way, moment, mid_rows, outer_columns)
         if more:
             links_y[state + 1][2].send()
 
@@ -647,17 +695,13 @@
         step(STEPS + turn, 1, STEPS - 1 - turn)
 
     for n, (h, a) in enumerate(blocks):
-        sig = gates[n]
         here = pl.ds(h * deep_y, deep_y)
         grad_mod = jnp.concatenate([totals[0, 4 * a + i, here] for i in range(4)], axis=0)
         grad_buoy = jnp.concatenate([totals[1, 4 * a + i, here] for i in range(4)], axis=0)
-        sig_speed, sig_dens = sig[: block // 2], sig[block // 2 :]
-        speed = 0.15 + 0.25 * sig_speed
-        density = 1.0 + 1.5 * sig_dens
-        grad_speed = grad_mod * 2.0 * density * speed
-        grad_dens = grad_mod * speed * speed - grad_buoy / (density * density)
-        gates[n, pl.ds(0, block // 2)] = grad_speed * 0.25 * sig_speed * (1.0 - sig_speed)
-        gates[n, pl.ds(block // 2, block // 2)] = grad_dens * 1.5 * sig_dens * (1.0 - sig_dens)
+        gates[n, pl.ds(0, block // 2)] = grad_mod * factors[0, n]
+        gates[n, pl.ds(block // 2, block // 2)] = (
+            grad_mod * factors[1, n] - grad_buoy * factors[2, n]
+        )
     permuted = mm(side_by_side(gates[...].reshape(len(blocks) * block, size_z)), from_depth)
     for n in range(len(blocks)):
         rows = jnp.transpose(permuted[n * block : (n + 1) * block])
@@ -669,8 +713,8 @@
     inner = split(
         mm3(outer, big_second, rows_by_rows) * (1.0 - hidden[...] * hidden[...])
     )
-    big_gf = mm3(split(jnp.transpose(latents[...])), inner)
-    big_gs = mm3(split(jnp.transpose(hidden[...])), outer)
+    big_gf = mm3((across[0, 0], across[0, 1]), inner)
+    big_gs = mm3((across[1, 0], across[1, 1]), outer)
     sum_f = 0.0
     sum_s = 0.0
     for b in range(GROUP):
@@ -833,7 +877,7 @@
     count = rec_pos.shape[2]
     anywhere = pl.BlockSpec(memory_space=pl.ANY)
     vmem = pl.BlockSpec(memory_space=pltpu.VMEM)
-    slots = (3 + PARTS) * 2 * STEPS + 3
+    slots = 6 * 2 * STEPS + 3
     piece = (CH + CH // 2) // shots
 
     def scratch(*shape, kind=jnp.float32):
@@ -862,6 +906,8 @@
             scratch(halves * rows_a * cells, GROUP * CH),
             scratch(halves * rows_a * cells, GROUP * CH),
             scratch(halves * rows_a, GROUP * outs // 4, size_z),
+            scratch(3, halves * rows_a, GROUP * outs // 8, size_z),
+            scratch(2, 2, GROUP * CH, halves * rows_a * cells, kind=half),
             scratch(*field),
             scratch(STEPS, *field),
             scratch((2 * STEPS + 1) * size_z, count, kind=half),

time: 55.6 us -> 54.5 us (0.980)
  Pallas kernels: 54.8 us -> 53.7 us
    pallas_call x1, Pallas kernels: 53.2 us -> 52.1 us  [body(): pl.pallas_call(whole_kernel, out_shape=(jax.ShapeDtypeStruct((rows_a, dep...]
where the time goes in v5:
time: 54.5 us; the launch traced here: 54.4 us
  Pallas kernels  53.7 us (99%)
  between operations  0.64 us (1%)
    pallas_call x1, Pallas kernels, body(): pl.pallas_call(whole_kernel, out_shape=(jax.ShapeDtypeStruct((rows_a, dep...  52.1 us
    pallas_call x1, Pallas kernels, body(): pl.pallas_call(finish_kernel, out_shape=(jax.ShapeDtypeStruct(own.shape,...  1.59 us

profile of v5, /device:TPU:0, one launch (start us, length us, event | category | flops | bytes accessed | tf_op | source)
XLA Modules:
  0.0 54.4 jit_solution(7184408227701352712)
XLA Ops:
  0.6 52.1 %shard_map.130 = (f32[6,8,512]{2,1,0:T(8,128)}, f32[4,24,128]{2,1,0:T(8,128)}) custom-call(f32[6,8,512]{2,1,0:T(8,128)} %bitcast.14, f32[64,64]{1,0:T(8,128)} %first_ref.1, f32[64,128]{1,0:T(8,128)} %second_ref.1, f32[24,32,128]{2,1,0:T(8,128)} %bitcast.12, f32[3,24,32,128]{3,2,1,0:T(8,128)} %bitcast.10, f32[24,32,128]{2,1,0:T(8,128)} %bitcast.13, ...), custom_call_target="tpu_custom_call" | custom-call | tf_op jit(solution)/shard_map/pallas_call | solution.py:889
  52.8 1.6 %shard_map.131 = (f32[6,8,512]{2,1,0:T(8,128)}, f32[64,64]{1,0:T(8,128)}, f32[64,128]{1,0:T(8,128)}) custom-call(f32[6,8,512]{2,1,0:T(8,128)} %get-tuple-element.8.own_ref, f32[4,24,128]{2,1,0:T(8,128)} %get-tuple-element.9.sums_ref), custom_call_target="tpu_custom_call" | custom-call | tf_op jit(solution)/shard_map/pallas_call | solution.py:962

commit v6 on v5

--- a/solution.py
+++ b/solution.py
@@ -644,9 +644,11 @@
     def step(state, way, moment):
         depth_part(state, way, moment)
         faces_x(state, way, moment, 3, size_x - 4, every)
-        if state < STEPS:
-            turns = size_x // chunk
-            lax.fori_loop(state * turns // STEPS, (state + 1) * turns // STEPS, planes, 0)
+        turns = size_x // chunk
+        if state == 0:
+            lax.fori_loop(0, 2 * turns // 3, planes, 0)
+        if state == 1:
+            lax.fori_loop(2 * turns // 3, turns, planes, 0)
         ends = [(0, low_rows, (-VRIM, 3)), (1, high_rows, (size_x - 4, size_x + 3))]
         if state % 2:
             ends.reverse()

time: 54.5 us -> 54.5 us (level)
  no operation moved by 1% of the time
where the time goes in v6:
time: 54.5 us; the launch traced here: 54.3 us
  Pallas kernels  53.7 us (99%)
  between operations  0.64 us (1%)
    pallas_call x1, Pallas kernels, body(): pl.pallas_call(whole_kernel, out_shape=(jax.ShapeDtypeStruct((rows_a, dep...  52.1 us
    pallas_call x1, Pallas kernels, body(): pl.pallas_call(finish_kernel, out_shape=(jax.ShapeDtypeStruct(own.shape,...  1.59 us

profile of v6, /device:TPU:0, one launch (start us, length us, event | category | flops | bytes accessed | tf_op | source)
XLA Modules:
  0.0 54.3 jit_solution(2424682310335597363)
XLA Ops:
  0.6 52.1 %shard_map.130 = (f32[6,8,512]{2,1,0:T(8,128)}, f32[4,24,128]{2,1,0:T(8,128)}) custom-call(f32[6,8,512]{2,1,0:T(8,128)} %bitcast.14, f32[64,64]{1,0:T(8,128)} %first_ref.1, f32[64,128]{1,0:T(8,128)} %second_ref.1, f32[24,32,128]{2,1,0:T(8,128)} %bitcast.12, f32[3,24,32,128]{3,2,1,0:T(8,128)} %bitcast.10, f32[24,32,128]{2,1,0:T(8,128)} %bitcast.13, ...), custom_call_target="tpu_custom_call" | custom-call | tf_op jit(solution)/shard_map/pallas_call | solution.py:891
  52.7 1.6 %shard_map.131 = (f32[6,8,512]{2,1,0:T(8,128)}, f32[64,64]{1,0:T(8,128)}, f32[64,128]{1,0:T(8,128)}) custom-call(f32[6,8,512]{2,1,0:T(8,128)} %get-tuple-element.8.own_ref, f32[4,24,128]{2,1,0:T(8,128)} %get-tuple-element.9.sums_ref), custom_call_target="tpu_custom_call" | custom-call | tf_op jit(solution)/shard_map/pallas_call | solution.py:964
